TPU v7x, 32 devices: a whole 2x2x4 slice. The times are simulated.
32 devices in a mesh: groups: 2 (over x), lon: 16 (over z, y, core).
Axes of the slice: x: 2, y: 2, z: 4, core: 2. Of those that a mesh axis runs over, the one named last changes fastest.
Arguments:
- queries: bfloat16 [32, 128, 2560], P('groups', 'lon'), parts along dimension 0, may hold values from -6 to 6
- keys_values: bfloat16 [2, 32, 128, 2560], P(None, 'groups', 'lon'), parts along dimension 1, may hold values from -6 to 6
- out_weight: bfloat16 [2560, 2560], replicated, may hold values from -0.47851562 to 0.47851562
- reg_queries: bfloat16 [128, 2560], P('groups'), parts along dimension 0, may hold values from -6 to 6
Outputs:
- attn_out: bfloat16 [32, 128, 2560], P('groups', 'lon'), parts along dimension 0
- reg_out: bfloat16 [128, 2560], P('groups'), parts along dimension 0
There are 2 independent parts, one for each index of `groups`. A program takes and returns all parts, laid end to end along the dimension named above; an argument that names none is the same for every part. Nothing has to cross between parts.
All inputs are finite; a program needn't handle non-finite values.
Results may differ from a plain program's by a relative error of at most 0.0057.
Values may be sent and summed in bfloat16 or wider, within the bound.
No kernel may reach another device: no remote copies, remote signals or barrier semaphores. Data moves between devices by JAX's collectives and lax.ppermute only.
A program may use at most 256 MiB of HBM per device.

v0:
```python
import functools
import math

import jax
import jax.numpy as jnp
from jax import lax
from jax.experimental import pallas as pl
from jax.experimental.pallas import tpu as pltpu
from jax.sharding import PartitionSpec as P


HEADS = 20
HEAD_DIM = 128
WIN = 7
RADIUS = WIN // 2
SCALE = math.log2(math.e) / math.sqrt(HEAD_DIM)
NEG = -1e30
GROUP = 32
CHUNKS = 4
BATCH = 4
MIB = 1 << 20


VMEM = pl.BlockSpec(memory_space=pltpu.VMEM)
SMEM = pl.BlockSpec(memory_space=pltpu.SMEM)
HBM = pl.BlockSpec(memory_space=pltpu.HBM)


def call(body, outs, flops, moved, exps=0, scratch=(), limit=8, space=VMEM):
    shapes = [jax.ShapeDtypeStruct(shape, dtype) for shape, dtype in outs]

    def run(*args):
        return pl.pallas_call(
            body,
            out_shape=shapes,
            in_specs=[SMEM] + [space] * (len(args) - 1),
            out_specs=[VMEM] * len(shapes),
            scratch_shapes=list(scratch),
            compiler_params=pltpu.CompilerParams(vmem_limit_bytes=limit * MIB),
            cost_estimate=pl.CostEstimate(flops=flops, bytes_accessed=moved, transcendentals=exps),
        )(*args)

    return run


def iota(shape, dim):
    return lax.broadcasted_iota(jnp.int32, shape, dim)


def mm(a, b, dims=((1,), (0,))):
    return lax.dot_general(a, b, (dims, ((), ())), preferred_element_type=jnp.float32)


def first_body(cols, place, kv_hbm, q_hbm, r_hbm, kv, q, near, far, keep, send, r, sems):
    tokens, width = q_hbm.shape
    rows = r_hbm.shape[0]
    half = rows // 2
    steps = HEADS // BATCH
    block = BATCH * HEAD_DIM
    copies = [pltpu.make_async_copy(r_hbm, r, sems.at[steps])]
    copies += [
        pltpu.make_async_copy(
            kv_hbm.at[:, :, pl.ds(step * block, block)],
            kv.at[:, :, pl.ds(step * block, block)],
            sems.at[step],
        )
        for step in range(steps)
    ]
    copies.append(pltpu.make_async_copy(q_hbm, q, sems.at[steps + 1]))
    for copy in copies:
        copy.start()
    bit = place[0] % 2
    count = tokens // cols * RADIUS
    row, token = iota((count, tokens), 0), iota((count, tokens), 1)
    base = row // RADIUS * cols + row % RADIUS
    high = cols - RADIUS
    pick_near = (token == base + jnp.where(bit == 1, 0, high)).astype(jnp.bfloat16)
    pick_far = (token == base + jnp.where(bit == 1, high, 0)).astype(jnp.bfloat16)
    pick = jnp.concatenate([pick_near, pick_far], axis=0)
    lane = iota((rows, HEAD_DIM), 1)
    peaks = jnp.zeros((rows, HEAD_DIM), jnp.float32)
    totals = jnp.zeros((rows, HEAD_DIM), jnp.float32)

    def store(value, at):
        low, high = value[:half], value[half:]
        keep[:, at] = jnp.where(bit == 0, low, high)
        send[:, at] = jnp.where(bit == 0, high, low).astype(send.dtype)

    copies[0].wait()
    for step in range(steps):
        copies[step + 1].wait()
        heads = range(step * BATCH, (step + 1) * BATCH)
        at = [slice(head * HEAD_DIM, (head + 1) * HEAD_DIM) for head in heads]
        scores = [mm(r[:, x], kv[0, :, x], ((1,), (1,))) * SCALE for x in at]
        whole = slice(step * block, (step + 1) * block)
        for part in range(2):
            picked = mm(pick, kv[part, :, whole]).astype(jnp.bfloat16)
            near[part, :, whole] = picked[:count]
            far[part, :, whole] = picked[count:]
        tops = [jnp.max(x, axis=-1, keepdims=True) for x in scores]
        tops = [x.astype(jnp.bfloat16).astype(jnp.float32) for x in tops]
        weights = [jnp.exp2(x - top) for x, top in zip(scores, tops)]
        parts = [jnp.sum(x, axis=-1, keepdims=True) for x in weights]
        sums = [mm(x.astype(jnp.bfloat16), kv[1, :, y]) for x, y in zip(weights, at)]
        for head, top, part, value, x in zip(heads, tops, parts, sums, at):
            peaks = jnp.where(lane == head, top, peaks)
            totals = jnp.where((lane == head + GROUP) | (lane == head + 2 * GROUP), part, totals)
            store(value, x)
    rounded = totals.astype(jnp.bfloat16).astype(jnp.float32)
    stats = jnp.where(lane < GROUP, peaks, jnp.where(lane < 2 * GROUP, rounded, totals - rounded))
    store(stats, slice(width, width + HEAD_DIM))
    copies[-1].wait()


def merge_body(level, split, last, place, mine, other, *outs):
    rows = mine.shape[0]
    lane = iota((rows, HEAD_DIM), 1)
    base = HEADS * HEAD_DIM
    a = mine[:, base:].astype(jnp.float32)
    b = other[:, base:].astype(jnp.float32)
    peak = jnp.maximum(a, b)
    ea, eb = jnp.exp2(a - peak), jnp.exp2(b - peak)

    def total_of(x):
        return pltpu.roll(x, HEAD_DIM - GROUP, 1) + pltpu.roll(x, HEAD_DIM - 2 * GROUP, 1)

    total = total_of(a) * ea + total_of(b) * eb
    pieces = []
    for head in range(HEADS):
        at = slice(head * HEAD_DIM, (head + 1) * HEAD_DIM)
        x = mine[:, at].astype(jnp.float32) * ea[:, head : head + 1]
        x = x + other[:, at].astype(jnp.float32) * eb[:, head : head + 1]
        if last:
            x = x / total[:, head : head + 1]
        pieces.append(x)
    if not last:
        total = jnp.where(lane < GROUP, total, 0.0)
        rounded = total.astype(jnp.bfloat16).astype(jnp.float32)
        stats = jnp.where(lane < GROUP, peak, 0.0)
        stats = stats + pltpu.roll(rounded, GROUP, 1) + pltpu.roll(total - rounded, 2 * GROUP, 1)
        pieces.append(stats)
    value = jnp.concatenate(pieces, axis=1)
    if not split:
        outs[0][...] = value.astype(outs[0].dtype)
        return
    keep, send = outs
    half = rows // 2
    bit = (place[0] // level) % 2

    @pl.when(bit == 0)
    def _():
        keep[...] = value[:half]
        send[...] = value[half:].astype(send.dtype)

    @pl.when(bit == 1)
    def _():
        keep[...] = value[half:]
        send[...] = value[:half].astype(send.dtype)


def attend_body(cols, first, count, place, q, kv, near, far, out):
    tokens = q.shape[0]
    rows = tokens // cols
    edge = rows * RADIUS
    keys = tokens + 2 * edge
    padded = -(-keys // 128) * 128
    odd = place[0] % 2
    shape = (tokens, padded)
    query, key = iota(shape, 0), iota(shape, 1)
    near_key, far_key = key - tokens, key - tokens - edge
    near_col = near_key % RADIUS + jnp.where(odd == 1, -RADIUS, cols)
    far_col = far_key % RADIUS + jnp.where(odd == 1, cols, -RADIUS)
    own = key < tokens
    mid = key < tokens + edge
    key_row = jnp.where(own, key // cols, jnp.where(mid, near_key // RADIUS, far_key // RADIUS))
    key_col = jnp.where(own, key % cols, jnp.where(mid, near_col, far_col))
    top = jnp.clip(query // cols - RADIUS, 0, rows - WIN)
    gap = key_col - query % cols
    inside = (key_row >= top) & (key_row < top + WIN) & (gap >= -RADIUS) & (gap <= RADIUS)
    bias = jnp.where(inside & (key < keys), 0.0, NEG)
    fill = jnp.zeros((padded - keys, HEAD_DIM), jnp.bfloat16)
    for index in range(count):
        head = first + index
        at = slice(head * HEAD_DIM, (head + 1) * HEAD_DIM)
        k = jnp.concatenate([kv[0, :, at], near[0, :, at], far[0, :, at], fill], axis=0)
        v = jnp.concatenate([kv[1, :, at], near[1, :, at], far[1, :, at], fill], axis=0)
        scores = mm(q[:, at], k, ((1,), (1,))) * SCALE + bias
        peak = jnp.max(scores, axis=-1, keepdims=True)
        weights = jnp.exp2(scores - peak)
        total = jnp.sum(weights, axis=-1, keepdims=True)
        blend = mm(weights.astype(jnp.bfloat16), v) / total
        out[:, index * HEAD_DIM : (index + 1) * HEAD_DIM] = blend.astype(jnp.bfloat16)


def join(out, start, bit, mine, other):
    rows = mine.shape[0]
    low, high = mine[...], other[...]
    out[start : start + rows] = jnp.where(bit == 0, low, high)
    out[start + rows : start + 2 * rows] = jnp.where(bit == 0, high, low)


def join_body(level, place, mine, other, out):
    join(out, 0, (place[0] // level) % 2, mine, other)


def project_body(place, mine, other, weight, *refs):
    blended, (out, reg_out), (x, projected) = refs[:-4], refs[-4:-2], refs[-2:]
    tokens = out.shape[0]
    width = weight.shape[0]
    start = 0
    for piece in blended:
        x[:tokens, start : start + piece.shape[1]] = piece[...]
        start += piece.shape[1]
    join(x, tokens, place[0] % 2, mine, other)
    block = 512
    square = jnp.zeros((reg_out.shape[0], 1), jnp.float32)
    for start in range(0, width, block):
        y = mm(x[...], weight[:, start : start + block])
        out[:, start : start + block] = y[:tokens].astype(jnp.bfloat16)
        r = y[tokens:]
        projected[:, start : start + block] = r
        square = square + jnp.sum(r * r, axis=-1, keepdims=True)
    scale = lax.rsqrt(square / width + 1e-06)
    reg_out[...] = (projected[...] * scale).astype(jnp.bfloat16)


def body(queries, keys_values, out_weight, reg_queries):
    latitudes, columns, model_width = queries.shape
    tokens = latitudes * columns
    bf16 = jnp.bfloat16
    size = lax.axis_size("lon")
    index = lax.axis_index("lon")
    place = jnp.reshape(index, (1,)).astype(jnp.int32)
    kv = keys_values.reshape(2, tokens, model_width)
    q = queries.reshape(tokens, model_width)
    edge = latitudes * RADIUS
    regs = reg_queries.shape[0]

    def exchange(x, pairs):
        return lax.ppermute(x, "lon", pairs)

    def flip(level):
        return [(i, i ^ level) for i in range(size)]

    pairs_far = [(i, (i + 1) % size if i % 2 else (i - 1) % size) for i in range(size)]

    wide = model_width + HEAD_DIM
    hbm = [pltpu.with_memory_space_constraint(x, pltpu.HBM) for x in (kv, q, reg_queries)]
    kv, q, near, far, keep, send = call(
        functools.partial(first_body, columns),
        [(kv.shape, bf16), (q.shape, bf16)]
        + [((2, edge, model_width), bf16)] * 2
        + [((regs // 2, wide), jnp.float32), ((regs // 2, wide), bf16)],
        flops=8 * edge * tokens * model_width + 4 * regs * tokens * model_width,
        moved=kv.size * 2,
        exps=regs * tokens * HEADS,
        scratch=(
            pltpu.VMEM(reg_queries.shape, bf16),
            pltpu.SemaphoreType.DMA((HEADS // BATCH + 2,)),
        ),
        space=HBM,
    )(place, *hbm)
    far_in = exchange(far, pairs_far)
    near_in = exchange(near, flip(1))

    levels = []
    level = 1
    while level < size:
        levels.append(level)
        level *= 2
    if len(levels) > 2:
        levels.append(levels.pop(1))
    halved = min(2, len(levels) - 1)
    other = exchange(send, flip(1))
    for step, level in enumerate(levels):
        split = step + 1 < halved
        last = step + 1 == len(levels)
        after = 0 if last else levels[step + 1]
        rows = keep.shape[0]
        shape = (rows // 2 if split else rows, model_width if last else wide)
        outs = call(
            functools.partial(merge_body, after, split, last),
            [(shape, jnp.float32), (shape, bf16)] if split else [(shape, bf16)],
            flops=rows * wide * 3,
            moved=rows * wide * 6,
        )(place, keep, other)
        if not last:
            keep = outs[0]
            other = exchange(outs[-1], flip(after))
    attended = outs[0]
    for step in range(halved - 1, -1, -1):
        other = exchange(attended, flip(levels[step]))
        if step:
            (attended,) = call(
                functools.partial(join_body, levels[step]),
                [((2 * attended.shape[0], model_width), bf16)],
                flops=attended.size,
                moved=attended.size * 8,
            )(place, attended, other)

    each = HEADS // CHUNKS
    blended = []
    for chunk in range(CHUNKS):
        (piece,) = call(
            functools.partial(attend_body, columns, chunk * each, each),
            [((tokens, each * HEAD_DIM), bf16)],
            flops=4 * tokens * 256 * each * HEAD_DIM,
            moved=tokens * each * HEAD_DIM * 12,
            exps=tokens * 256 * each,
        )(place, q, kv, near_in, far_in)
        blended.append(piece)

    attn_out, reg_out = call(
        project_body,
        [((tokens, model_width), bf16), ((regs, model_width), bf16)],
        flops=2 * (tokens + regs) * model_width * model_width,
        moved=2 * model_width * model_width,
        scratch=(
            pltpu.VMEM((tokens + regs, model_width), bf16),
            pltpu.VMEM((regs, model_width), jnp.float32),
        ),
        limit=16,
    )(place, attended, other, out_weight, *blended)
    return (attn_out.reshape(latitudes, columns, model_width), reg_out)


def solution(mesh):
    in_specs = (P("groups", "lon", None), P(None, "groups", "lon", None), P(), P("groups", None))
    out_specs = (P("groups", "lon", None), P("groups", None))
    return jax.shard_map(body, mesh=mesh, in_specs=in_specs, out_specs=out_specs, check_vma=False)
```

profile of v0, /device:TPU:0, one launch (start us, length us, event | category | flops | bytes accessed | tf_op | source)
XLA Modules:
  0.0 43.0 jit_solution(13983404251098838638)
XLA Ops:
  0.6 3.3 %shard_map.59 = (bf16[2,128,2560]{2,1,0:T(8,128)(2,1)S(1)}, bf16[128,2560]{1,0:T(8,128)(2,1)S(1)}, bf16[2,48,2560]{2,1,0:T(8,128)(2,1)S(1)}, bf16[2,48,2560]{2,1...) custom-call(s32[1]{0:T(128)} %bitcast.place, bf16[2,128,2560]{2,1,0:T(8,128)(2,1)} %bitcast.4, ...), custom_call_target="tpu_custom_call" | custom-call | flops 209715200 | bytes 1310720 | tf_op jit(solution)/shard_map/pallas_call | solution.py:33
  3.9 0.6 %collective-permute-start = (bf16[32,2688]{1,0:T(8,128)(2,1)S(1)}, bf16[32,2688]{1,0:T(8,128)(2,1)S(1)}, u32[]{:S(2)}, u32[]{:S(2)}) collective-permute-start(bf16[32,2688]{1,0:T(8,128)(2,1)S(1)} %get-tuple-element.13), channel_id=1, source_target_pairs={{0,1},{1,0},{2,3},{3,2},{4,5},{5,4},{6,7},{7,6},{8,9},{9,8},{10,11... | collective-permute-start | bytes 516104 | tf_op jit(solution)/shard_map/ppermute | solution.py:240
  4.5 0.1 collective-permute-start.6
  4.6 5.7 %collective-permute-start.7 = (bf16[2,48,2560]{2,1,0:T(8,128)(2,1)S(1)}, bf16[2,48,2560]{2,1,0:T(8,128)(2,1)S(1)}, u32[]{:S(2)}, u32[]{:S(2)}) collective-permute-start(bf16[2,48,2560]{2,1,0:T(8,128)(2,1)S(1)} %get-tuple-element.19), channel_id=1, source_target_pairs={{0,15},{1,2},{2,1},{3,4},{4,3},{5,6},{6,5},{7,8},{8,7},{9,10},{10,... | collective-permute-start | bytes 1474568 | tf_op jit(solution)/shard_map/ppermute | solution.py:240
  10.2 0.0 collective-permute-done.other
  10.2 0.3 shard_map.60
  10.5 0.1 collective-permute-start.1
  10.6 7.9 %collective-permute-done.1.other = bf16[16,2688]{1,0:T(8,128)(2,1)S(1)} collective-permute-done((bf16[16,2688]{1,0:T(8,128)(2,1)S(1)}, bf16[16,2688]{1,0:T(8,128)(2,1)S(1)}, u32[]{:S(2)}, u32[]{:S(2)}) %collective-permute-start.1) | collective-permute-done | bytes 86048 | tf_op jit(solution)/shard_map/ppermute | solution.py:240
  18.5 0.2 shard_map.61.mine
  18.7 2.4 %collective-permute-start.2 = (bf16[16,2688]{1,0:T(8,128)(2,1)S(1)}, bf16[16,2688]{1,0:T(8,128)(2,1)S(1)}, u32[]{:S(2)}, u32[]{:S(2)}) collective-permute-start(bf16[16,2688]{1,0:T(8,128)(2,1)S(1)} %shard_map.61.mine), channel_id=1, source_target_pairs={{0,8},{1,9},{2,10},{3,11},{4,12},{5,13},{6,14},{7,15},{8,0},{9,1},... | collective-permute-start | bytes 258056 | tf_op jit(solution)/shard_map/ppermute | solution.py:240
  21.1 3.1 %collective-permute-done.2.other = bf16[16,2688]{1,0:T(8,128)(2,1)S(1)} collective-permute-done((bf16[16,2688]{1,0:T(8,128)(2,1)S(1)}, bf16[16,2688]{1,0:T(8,128)(2,1)S(1)}, u32[]{:S(2)}, u32[]{:S(2)}) %collective-permute-start.2) | collective-permute-done | bytes 86048 | tf_op jit(solution)/shard_map/ppermute | solution.py:240
  24.1 0.0 copy-start
  24.2 0.2 shard_map.62.mine
  24.3 2.1 %collective-permute-start.3 = (bf16[16,2688]{1,0:T(8,128)(2,1)S(1)}, bf16[16,2688]{1,0:T(8,128)(2,1)S(1)}, u32[]{:S(2)}, u32[]{:S(2)}) collective-permute-start(bf16[16,2688]{1,0:T(8,128)(2,1)S(1)} %shard_map.62.mine), channel_id=1, source_target_pairs={{0,2},{1,3},{2,0},{3,1},{4,6},{5,7},{6,4},{7,5},{8,10},{9,11},{10,... | collective-permute-start | bytes 258056 | tf_op jit(solution)/shard_map/ppermute | solution.py:240
  26.4 2.7 %collective-permute-done.3.other = bf16[16,2688]{1,0:T(8,128)(2,1)S(1)} collective-permute-done((bf16[16,2688]{1,0:T(8,128)(2,1)S(1)}, bf16[16,2688]{1,0:T(8,128)(2,1)S(1)}, u32[]{:S(2)}, u32[]{:S(2)}) %collective-permute-start.3) | collective-permute-done | bytes 86048 | tf_op jit(solution)/shard_map/ppermute | solution.py:240
  29.2 0.3 shard_map.63.mine
  29.4 2.3 %collective-permute-start.4 = (bf16[16,2560]{1,0:T(8,128)(2,1)S(1)}, bf16[16,2560]{1,0:T(8,128)(2,1)S(1)}, u32[]{:S(2)}, u32[]{:S(2)}) collective-permute-start(bf16[16,2560]{1,0:T(8,128)(2,1)S(1)} %shard_map.63.mine), channel_id=1, source_target_pairs={{0,4},{1,5},{2,6},{3,7},{4,0},{5,1},{6,2},{7,3},{8,12},{9,13},{10,... | collective-permute-start | bytes 245768 | tf_op jit(solution)/shard_map/ppermute | solution.py:240
  31.7 2.4 %collective-permute-done.4.other = bf16[16,2560]{1,0:T(8,128)(2,1)S(1)} collective-permute-done((bf16[16,2560]{1,0:T(8,128)(2,1)S(1)}, bf16[16,2560]{1,0:T(8,128)(2,1)S(1)}, u32[]{:S(2)}, u32[]{:S(2)}) %collective-permute-start.4) | collective-permute-done | bytes 81952 | tf_op jit(solution)/shard_map/ppermute | solution.py:240
  34.2 0.1 collective-permute-start.5
  34.2 0.0 collective-permute-done.6.near
  34.2 0.0 collective-permute-done.7.far
  34.3 1.3 %shard_map.68.refs_3_ = bf16[128,640]{1,0:T(8,128)(2,1)S(1)} custom-call(s32[1]{0:T(128)} %bitcast.place, bf16[128,2560]{1,0:T(8,128)(2,1)S(1)} %get-tuple-element.16.q, bf16[2,128,2560]{2,1,0:T(8,128)(2,1)S(1)} %get-tuple-element.17.kv, bf16[2,48,2560]{2,1,0:T(8,128)(2,1)S(1)} %collective-permute-done.6.near, ...), custom_call_target="tpu_custom_call" | custom-call | flops 83886080 | bytes 983040 | tf_op jit(solution)/shard_map/pallas_call | solution.py:33
  35.5 1.3 %shard_map.67.refs_2_ = bf16[128,640]{1,0:T(8,128)(2,1)S(1)} custom-call(s32[1]{0:T(128)} %bitcast.place, bf16[128,2560]{1,0:T(8,128)(2,1)S(1)} %get-tuple-element.16.q, bf16[2,128,2560]{2,1,0:T(8,128)(2,1)S(1)} %get-tuple-element.17.kv, bf16[2,48,2560]{2,1,0:T(8,128)(2,1)S(1)} %collective-permute-done.6.near, ...), custom_call_target="tpu_custom_call" | custom-call | flops 83886080 | bytes 983040 | tf_op jit(solution)/shard_map/pallas_call | solution.py:33
  36.8 1.3 %shard_map.66.refs_1_ = bf16[128,640]{1,0:T(8,128)(2,1)S(1)} custom-call(s32[1]{0:T(128)} %bitcast.place, bf16[128,2560]{1,0:T(8,128)(2,1)S(1)} %get-tuple-element.16.q, bf16[2,128,2560]{2,1,0:T(8,128)(2,1)S(1)} %get-tuple-element.17.kv, bf16[2,48,2560]{2,1,0:T(8,128)(2,1)S(1)} %collective-permute-done.6.near, ...), custom_call_target="tpu_custom_call" | custom-call | flops 83886080 | bytes 983040 | tf_op jit(solution)/shard_map/pallas_call | solution.py:33
  38.1 1.3 %shard_map.65.refs_0_ = bf16[128,640]{1,0:T(8,128)(2,1)S(1)} custom-call(s32[1]{0:T(128)} %bitcast.place, bf16[128,2560]{1,0:T(8,128)(2,1)S(1)} %get-tuple-element.16.q, bf16[2,128,2560]{2,1,0:T(8,128)(2,1)S(1)} %get-tuple-element.17.kv, bf16[2,48,2560]{2,1,0:T(8,128)(2,1)S(1)} %collective-permute-done.6.near, ...), custom_call_target="tpu_custom_call" | custom-call | flops 83886080 | bytes 983040 | tf_op jit(solution)/shard_map/pallas_call | solution.py:33
  39.4 0.0 collective-permute-done.5.other
  39.4 0.0 copy-done
  39.4 3.7 %shard_map.69 = (bf16[128,2560]{1,0:T(8,128)(2,1)}, bf16[64,2560]{1,0:T(8,128)(2,1)}) custom-call(s32[1]{0:T(128)} %bitcast.place, bf16[32,2560]{1,0:T(8,128)(2,1)S(1)} %shard_map.64.mine, bf16[32,2560]{1,0:T(8,128)(2,1)S(1)} %collective-permute-done.5.other, bf16[2560,2560]{1,0:T(8,128)(2,1)S(1)} %copy-done, bf16[128,640]{1,0:T(8,128)(2,1)S(1)} %shard_map.65.refs_0_, ...), custom_call_target="tpu_custom_call" | custom-call | flops 2516582400 | bytes 13107200 | tf_op jit(solution)/shard_map/pallas_call | solution.py:33
  (1 shorter events, 0.0 us)
Async XLA Ops:
  3.9 6.3 %collective-permute-start = (bf16[32,2688]{1,0:T(8,128)(2,1)S(1)}, bf16[32,2688]{1,0:T(8,128)(2,1)S(1)}, u32[]{:S(2)}, u32[]{:S(2)}) collective-permute-start(bf16[32,2688]{1,0:T(8,128)(2,1)S(1)} %get-tuple-element.13), channel_id=1, source_target_pairs={{0,1},{1,0},{2,3},{3,2},{4,5},{5,4},{6,7},{7,6},{8,9},{9,8},{10,11... | collective-permute-start | bytes 516104 | tf_op jit(solution)/shard_map/ppermute | solution.py:240
  4.5 29.7 %collective-permute-start.6 = (bf16[2,48,2560]{2,1,0:T(8,128)(2,1)S(1)}, bf16[2,48,2560]{2,1,0:T(8,128)(2,1)S(1)}, u32[]{:S(2)}, u32[]{:S(2)}) collective-permute-start(bf16[2,48,2560]{2,1,0:T(8,128)(2,1)S(1)} %get-tuple-element.18), channel_id=1, source_target_pairs={{0,1},{1,0},{2,3},{3,2},{4,5},{5,4},{6,7},{7,6},{8,9},{9,8},{10,11... | collective-permute-start | bytes 1474568 | tf_op jit(solution)/shard_map/ppermute | solution.py:240
  4.6 29.7 %collective-permute-start.7 = (bf16[2,48,2560]{2,1,0:T(8,128)(2,1)S(1)}, bf16[2,48,2560]{2,1,0:T(8,128)(2,1)S(1)}, u32[]{:S(2)}, u32[]{:S(2)}) collective-permute-start(bf16[2,48,2560]{2,1,0:T(8,128)(2,1)S(1)} %get-tuple-element.19), channel_id=1, source_target_pairs={{0,15},{1,2},{2,1},{3,4},{4,3},{5,6},{6,5},{7,8},{8,7},{9,10},{10,... | collective-permute-start | bytes 1474568 | tf_op jit(solution)/shard_map/ppermute | solution.py:240
  10.5 8.0 %collective-permute-start.1 = (bf16[16,2688]{1,0:T(8,128)(2,1)S(1)}, bf16[16,2688]{1,0:T(8,128)(2,1)S(1)}, u32[]{:S(2)}, u32[]{:S(2)}) collective-permute-start(bf16[16,2688]{1,0:T(8,128)(2,1)S(1)} %get-tuple-element.15), channel_id=1, source_target_pairs={{0,4},{1,5},{2,6},{3,7},{4,0},{5,1},{6,2},{7,3},{8,12},{9,13},{10,... | collective-permute-start | bytes 258056 | tf_op jit(solution)/shard_map/ppermute | solution.py:240
  18.7 5.4 %collective-permute-start.2 = (bf16[16,2688]{1,0:T(8,128)(2,1)S(1)}, bf16[16,2688]{1,0:T(8,128)(2,1)S(1)}, u32[]{:S(2)}, u32[]{:S(2)}) collective-permute-start(bf16[16,2688]{1,0:T(8,128)(2,1)S(1)} %shard_map.61.mine), channel_id=1, source_target_pairs={{0,8},{1,9},{2,10},{3,11},{4,12},{5,13},{6,14},{7,15},{8,0},{9,1},... | collective-permute-start | bytes 258056 | tf_op jit(solution)/shard_map/ppermute | solution.py:240
  24.1 15.2 %copy-start = (bf16[2560,2560]{1,0:T(8,128)(2,1)S(1)}, bf16[2560,2560]{1,0:T(8,128)(2,1)}, u32[]{:S(2)}) copy-start(bf16[2560,2560]{1,0:T(8,128)(2,1)} %weight.1) | copy-start | bytes 39321604
  24.3 4.8 %collective-permute-start.3 = (bf16[16,2688]{1,0:T(8,128)(2,1)S(1)}, bf16[16,2688]{1,0:T(8,128)(2,1)S(1)}, u32[]{:S(2)}, u32[]{:S(2)}) collective-permute-start(bf16[16,2688]{1,0:T(8,128)(2,1)S(1)} %shard_map.62.mine), channel_id=1, source_target_pairs={{0,2},{1,3},{2,0},{3,1},{4,6},{5,7},{6,4},{7,5},{8,10},{9,11},{10,... | collective-permute-start | bytes 258056 | tf_op jit(solution)/shard_map/ppermute | solution.py:240
  29.4 4.7 %collective-permute-start.4 = (bf16[16,2560]{1,0:T(8,128)(2,1)S(1)}, bf16[16,2560]{1,0:T(8,128)(2,1)S(1)}, u32[]{:S(2)}, u32[]{:S(2)}) collective-permute-start(bf16[16,2560]{1,0:T(8,128)(2,1)S(1)} %shard_map.63.mine), channel_id=1, source_target_pairs={{0,4},{1,5},{2,6},{3,7},{4,0},{5,1},{6,2},{7,3},{8,12},{9,13},{10,... | collective-permute-start | bytes 245768 | tf_op jit(solution)/shard_map/ppermute | solution.py:240
  34.2 5.2 %collective-permute-start.5 = (bf16[32,2560]{1,0:T(8,128)(2,1)S(1)}, bf16[32,2560]{1,0:T(8,128)(2,1)S(1)}, u32[]{:S(2)}, u32[]{:S(2)}) collective-permute-start(bf16[32,2560]{1,0:T(8,128)(2,1)S(1)} %shard_map.64.mine), channel_id=1, source_target_pairs={{0,1},{1,0},{2,3},{3,2},{4,5},{5,4},{6,7},{7,6},{8,9},{9,8},{10,11... | collective-permute-start | bytes 491528 | tf_op jit(solution)/shard_map/ppermute | solution.py:240
where the time goes:
time: 43.2 us; the launch traced here: 43 us
  waiting for transfers between devices  16.1 us (37%)
  starting transfers between devices  13.2 us (31%)
  Pallas kernels  13 us (30%)
  between operations  0.73 us (2%)
    ppermute x8, waiting for transfers between devices, exchange(): return lax.ppermute(x, 'lon', pairs)  16.1 us
    ppermute x8, starting transfers between devices, exchange(): return lax.ppermute(x, 'lon', pairs)  13.2 us
    pallas_call x11, Pallas kernels, run(): pl.pallas_call(body, out_shape=shapes, in_specs=[SMEM] + [space] * (len(a...  13 us
  transfers between devices with their start and end apart: 8, of which 4 were waited for; matrix products, arithmetic and copies ran while one was open for 0% of the time, Pallas kernels for 14%

commit v1 on v0

--- a/solution.py
+++ b/solution.py
@@ -16,8 +16,11 @@
 SCALE = math.log2(math.e) / math.sqrt(HEAD_DIM)
 NEG = -1e30
 GROUP = 32
-CHUNKS = 4
-BATCH = 4
+CHUNKS = 1
+BATCH = 10
+ABATCH = 5
+PIECES = 2
+LOADS = 2
 MIB = 1 << 20
 
 
@@ -51,8 +54,20 @@
     return lax.dot_general(a, b, (dims, ((), ())), preferred_element_type=jnp.float32)
 
 
-def first_body(cols, place, kv_hbm, q_hbm, r_hbm, kv, q, near, far, keep, send, r, sems):
-    tokens, width = q_hbm.shape
+def place_of(part, start, width):
+    span = width * 2 // PIECES
+    return part * (PIECES // 2) + start // span, start % span
+
+
+def spread(far, part, start, value):
+    for low in range(0, value.shape[1], HEAD_DIM):
+        piece, at = place_of(part, start + low, HEADS * HEAD_DIM)
+        far[piece][:, at : at + HEAD_DIM] = value[:, low : low + HEAD_DIM]
+
+
+def first_body(cols, place, kv_hbm, r_hbm, kv, near, keep, send, *refs):
+    far, (r, sems) = refs[:-2], refs[-2:]
+    tokens, width = kv_hbm.shape[1:]
     rows = r_hbm.shape[0]
     half = rows // 2
     steps = HEADS // BATCH
@@ -66,7 +81,6 @@
         )
         for step in range(steps)
     ]
-    copies.append(pltpu.make_async_copy(q_hbm, q, sems.at[steps + 1]))
     for copy in copies:
         copy.start()
     bit = place[0] % 2
@@ -96,7 +110,7 @@
         for part in range(2):
             picked = mm(pick, kv[part, :, whole]).astype(jnp.bfloat16)
             near[part, :, whole] = picked[:count]
-            far[part, :, whole] = picked[count:]
+            spread(far, part, step * block, picked[count:])
         tops = [jnp.max(x, axis=-1, keepdims=True) for x in scores]
         tops = [x.astype(jnp.bfloat16).astype(jnp.float32) for x in tops]
         weights = [jnp.exp2(x - top) for x, top in zip(scores, tops)]
@@ -109,7 +123,6 @@
     rounded = totals.astype(jnp.bfloat16).astype(jnp.float32)
     stats = jnp.where(lane < GROUP, peaks, jnp.where(lane < 2 * GROUP, rounded, totals - rounded))
     store(stats, slice(width, width + HEAD_DIM))
-    copies[-1].wait()
 
 
 def merge_body(level, split, last, place, mine, other, *outs):
@@ -158,7 +171,8 @@
         send[...] = value[:half].astype(send.dtype)
 
 
-def attend_body(cols, first, count, place, q, kv, near, far, out):
+def attend_body(cols, first, count, place, q, kv, near, *refs):
+    far, out = refs[:-1], refs[-1]
     tokens = q.shape[0]
     rows = tokens // cols
     edge = rows * RADIUS
@@ -179,17 +193,23 @@
     inside = (key_row >= top) & (key_row < top + WIN) & (gap >= -RADIUS) & (gap <= RADIUS)
     bias = jnp.where(inside & (key < keys), 0.0, NEG)
     fill = jnp.zeros((padded - keys, HEAD_DIM), jnp.bfloat16)
-    for index in range(count):
-        head = first + index
-        at = slice(head * HEAD_DIM, (head + 1) * HEAD_DIM)
-        k = jnp.concatenate([kv[0, :, at], near[0, :, at], far[0, :, at], fill], axis=0)
-        v = jnp.concatenate([kv[1, :, at], near[1, :, at], far[1, :, at], fill], axis=0)
-        scores = mm(q[:, at], k, ((1,), (1,))) * SCALE + bias
-        peak = jnp.max(scores, axis=-1, keepdims=True)
-        weights = jnp.exp2(scores - peak)
-        total = jnp.sum(weights, axis=-1, keepdims=True)
-        blend = mm(weights.astype(jnp.bfloat16), v) / total
-        out[:, index * HEAD_DIM : (index + 1) * HEAD_DIM] = blend.astype(jnp.bfloat16)
+
+    def keys_of(part, at):
+        piece, start = place_of(part, at.start, kv.shape[2])
+        side = far[piece][:, start : start + HEAD_DIM]
+        return jnp.concatenate([kv[part, :, at], near[part, :, at], side, fill], axis=0)
+
+    for low in range(0, count, ABATCH):
+        span = range(low, min(low + ABATCH, count))
+        ats = [slice((first + i) * HEAD_DIM, (first + i + 1) * HEAD_DIM) for i in span]
+        scores = [mm(q[:, at], keys_of(0, at), ((1,), (1,))) for at in ats]
+        scores = [x * SCALE + bias for x in scores]
+        peaks = [jnp.max(x, axis=-1, keepdims=True) for x in scores]
+        weights = [jnp.exp2(x - peak) for x, peak in zip(scores, peaks)]
+        totals = [jnp.sum(x, axis=-1, keepdims=True) for x in weights]
+        sums = [mm(x.astype(jnp.bfloat16), keys_of(1, at)) for x, at in zip(weights, ats)]
+        for i, x, total in zip(span, sums, totals):
+            out[:, i * HEAD_DIM : (i + 1) * HEAD_DIM] = (x / total).astype(jnp.bfloat16)
 
 
 def join(out, start, bit, mine, other):
@@ -203,19 +223,29 @@
     join(out, 0, (place[0] // level) % 2, mine, other)
 
 
-def project_body(place, mine, other, weight, *refs):
-    blended, (out, reg_out), (x, projected) = refs[:-4], refs[-4:-2], refs[-2:]
+def load_body(part, place, source, target, sem):
+    columns = target.shape[1]
+    copy = pltpu.make_async_copy(source.at[:, pl.ds(part * columns, columns)], target, sem)
+    copy.start()
+    copy.wait()
+
+
+def project_body(place, mine, other, *refs):
+    weights, blended = refs[:LOADS], refs[LOADS:-4]
+    (out, reg_out), (x, projected) = refs[-4:-2], refs[-2:]
     tokens = out.shape[0]
-    width = weight.shape[0]
+    width = out.shape[1]
     start = 0
     for piece in blended:
         x[:tokens, start : start + piece.shape[1]] = piece[...]
         start += piece.shape[1]
     join(x, tokens, place[0] % 2, mine, other)
-    block = 512
+    span = weights[0].shape[1]
+    block = math.gcd(span, 512)
     square = jnp.zeros((reg_out.shape[0], 1), jnp.float32)
     for start in range(0, width, block):
-        y = mm(x[...], weight[:, start : start + block])
+        low = start % span
+        y = mm(x[...], weights[start // span][:, low : low + block])
         out[:, start : start + block] = y[:tokens].astype(jnp.bfloat16)
         r = y[tokens:]
         projected[:, start : start + block] = r
@@ -245,22 +275,24 @@
     pairs_far = [(i, (i + 1) % size if i % 2 else (i - 1) % size) for i in range(size)]
 
     wide = model_width + HEAD_DIM
-    hbm = [pltpu.with_memory_space_constraint(x, pltpu.HBM) for x in (kv, q, reg_queries)]
-    kv, q, near, far, keep, send = call(
+    hbm = [pltpu.with_memory_space_constraint(x, pltpu.HBM) for x in (kv, reg_queries)]
+    kv, near, keep, send, *far = call(
         functools.partial(first_body, columns),
-        [(kv.shape, bf16), (q.shape, bf16)]
-        + [((2, edge, model_width), bf16)] * 2
-        + [((regs // 2, wide), jnp.float32), ((regs // 2, wide), bf16)],
+        [(kv.shape, bf16), ((2, edge, model_width), bf16)]
+        + [((regs // 2, wide), jnp.float32), ((regs // 2, wide), bf16)]
+        + [((edge, 2 * model_width // PIECES), bf16)] * PIECES,
         flops=8 * edge * tokens * model_width + 4 * regs * tokens * model_width,
         moved=kv.size * 2,
         exps=regs * tokens * HEADS,
         scratch=(
             pltpu.VMEM(reg_queries.shape, bf16),
-            pltpu.SemaphoreType.DMA((HEADS // BATCH + 2,)),
+            pltpu.SemaphoreType.DMA((HEADS // BATCH + 1,)),
         ),
         space=HBM,
     )(place, *hbm)
-    far_in = exchange(far, pairs_far)
+    far_in = []
+    for piece in range(PIECES):
+        far_in.append(exchange(far[piece], pairs_far))
     near_in = exchange(near, flip(1))
 
     levels = []
@@ -307,8 +339,20 @@
             flops=4 * tokens * 256 * each * HEAD_DIM,
             moved=tokens * each * HEAD_DIM * 12,
             exps=tokens * 256 * each,
-        )(place, q, kv, near_in, far_in)
+        )(place, q, kv, near_in, *far_in)
         blended.append(piece)
+
+    weight_hbm = pltpu.with_memory_space_constraint(out_weight, pltpu.HBM)
+    weights = []
+    for part in range(LOADS):
+        weights += call(
+            functools.partial(load_body, part),
+            [((model_width, model_width // LOADS), bf16)],
+            flops=1,
+            moved=4 * model_width * model_width // LOADS,
+            scratch=(pltpu.SemaphoreType.DMA,),
+            space=HBM,
+        )(place, weight_hbm)
 
     attn_out, reg_out = call(
         project_body,
@@ -320,7 +364,7 @@
             pltpu.VMEM((regs, model_width), jnp.float32),
         ),
         limit=16,
-    )(place, attended, other, out_weight, *blended)
+    )(place, attended, other, *weights, *blended)
     return (attn_out.reshape(latitudes, columns, model_width), reg_out)
 
 

time: 43.2 us -> 44.2 us (1.023)
  Pallas kernels: 13 us -> 14.5 us
  waiting for transfers between devices: 16.1 us -> 15.4 us
    pallas_call x11 -> x10, Pallas kernels: 13 us -> 14.5 us  [run(): pl.pallas_call(body, out_shape=shapes, in_specs=[SMEM] + [space] * (len(a...]
    ppermute x8 -> x9, waiting for transfers between devices: 16.1 us -> 15.4 us  [exchange(): return lax.ppermute(x, 'lon', pairs)]
    ppermute x8 -> x9, starting transfers between devices: 13.2 us -> 13.2 us  [exchange(): return lax.ppermute(x, 'lon', pairs)]
  transfers between devices with their start and end apart: 8 -> 9, of which waited for: 4 -> 5; matrix products, arithmetic and copies ran while one was open for 0% -> 0% of each run, Pallas kernels for 14% -> 19%
where the time goes in v1:
time: 44.2 us; the launch traced here: 43.9 us
  waiting for transfers between devices  15.4 us (35%)
  Pallas kernels  14.5 us (33%)
  starting transfers between devices  13.2 us (30%)
  between operations  0.75 us (2%)
    ppermute x9, waiting for transfers between devices, exchange(): return lax.ppermute(x, 'lon', pairs)  15.4 us
    pallas_call x10, Pallas kernels, run(): pl.pallas_call(body, out_shape=shapes, in_specs=[SMEM] + [space] * (len(a...  14.5 us
    ppermute x9, starting transfers between devices, exchange(): return lax.ppermute(x, 'lon', pairs)  13.2 us
  transfers between devices with their start and end apart: 9, of which 5 were waited for; matrix products, arithmetic and copies ran while one was open for 0% of the time, Pallas kernels for 19%

profile of v1, /device:TPU:0, one launch (start us, length us, event | category | flops | bytes accessed | tf_op | source)
XLA Modules:
  0.0 43.9 jit_solution(2528590800946639961)
XLA Ops:
  0.6 2.4 %shard_map.59 = (bf16[2,128,2560]{2,1,0:T(8,128)(2,1)S(1)}, bf16[2,48,2560]{2,1,0:T(8,128)(2,1)S(1)}, f32[32,2688]{1,0:T(8,128)S(1)}, bf16[32,2688]{1,0:T(8,128)...) custom-call(s32[1]{0:T(128)} %bitcast.place, bf16[2,128,2560]{2,1,0:T(8,128)(2,1)} %bitcast.5, ...), custom_call_target="tpu_custom_call" | custom-call | flops 209715200 | bytes 1310720 | tf_op jit(solution)/shard_map/pallas_call | solution.py:36
  3.0 0.6 %collective-permute-start = (bf16[32,2688]{1,0:T(8,128)(2,1)S(1)}, bf16[32,2688]{1,0:T(8,128)(2,1)S(1)}, u32[]{:S(2)}, u32[]{:S(2)}) collective-permute-start(bf16[32,2688]{1,0:T(8,128)(2,1)S(1)} %get-tuple-element.13), channel_id=1, source_target_pairs={{0,1},{1,0},{2,3},{3,2},{4,5},{5,4},{6,7},{7,6},{8,9},{9,8},{10,11... | collective-permute-start | bytes 516104 | tf_op jit(solution)/shard_map/ppermute | solution.py:270
  3.6 0.1 collective-permute-start.6
  3.7 1.0 %collective-permute-done.other = bf16[32,2688]{1,0:T(8,128)(2,1)S(1)} collective-permute-done((bf16[32,2688]{1,0:T(8,128)(2,1)S(1)}, bf16[32,2688]{1,0:T(8,128)(2,1)S(1)}, u32[]{:S(2)}, u32[]{:S(2)}) %collective-permute-start) | collective-permute-done | bytes 172064 | tf_op jit(solution)/shard_map/ppermute | solution.py:270
  4.6 0.3 shard_map.60
  4.9 3.0 %collective-permute-start.1 = (bf16[16,2688]{1,0:T(8,128)(2,1)S(1)}, bf16[16,2688]{1,0:T(8,128)(2,1)S(1)}, u32[]{:S(2)}, u32[]{:S(2)}) collective-permute-start(bf16[16,2688]{1,0:T(8,128)(2,1)S(1)} %get-tuple-element.15), channel_id=1, source_target_pairs={{0,4},{1,5},{2,6},{3,7},{4,0},{5,1},{6,2},{7,3},{8,12},{9,13},{10,... | collective-permute-start | bytes 258056 | tf_op jit(solution)/shard_map/ppermute | solution.py:270
  7.9 2.8 %collective-permute-done.1.other = bf16[16,2688]{1,0:T(8,128)(2,1)S(1)} collective-permute-done((bf16[16,2688]{1,0:T(8,128)(2,1)S(1)}, bf16[16,2688]{1,0:T(8,128)(2,1)S(1)}, u32[]{:S(2)}, u32[]{:S(2)}) %collective-permute-start.1) | collective-permute-done | bytes 86048 | tf_op jit(solution)/shard_map/ppermute | solution.py:270
  10.8 0.2 shard_map.61.mine
  11.0 2.8 %collective-permute-start.2 = (bf16[16,2688]{1,0:T(8,128)(2,1)S(1)}, bf16[16,2688]{1,0:T(8,128)(2,1)S(1)}, u32[]{:S(2)}, u32[]{:S(2)}) collective-permute-start(bf16[16,2688]{1,0:T(8,128)(2,1)S(1)} %shard_map.61.mine), channel_id=1, source_target_pairs={{0,8},{1,9},{2,10},{3,11},{4,12},{5,13},{6,14},{7,15},{8,0},{9,1},... | collective-permute-start | bytes 258056 | tf_op jit(solution)/shard_map/ppermute | solution.py:270
  13.8 4.0 %collective-permute-done.2.other = bf16[16,2688]{1,0:T(8,128)(2,1)S(1)} collective-permute-done((bf16[16,2688]{1,0:T(8,128)(2,1)S(1)}, bf16[16,2688]{1,0:T(8,128)(2,1)S(1)}, u32[]{:S(2)}, u32[]{:S(2)}) %collective-permute-start.2) | collective-permute-done | bytes 86048 | tf_op jit(solution)/shard_map/ppermute | solution.py:270
  17.8 0.2 shard_map.62.mine
  18.0 1.6 %collective-permute-start.3 = (bf16[16,2688]{1,0:T(8,128)(2,1)S(1)}, bf16[16,2688]{1,0:T(8,128)(2,1)S(1)}, u32[]{:S(2)}, u32[]{:S(2)}) collective-permute-start(bf16[16,2688]{1,0:T(8,128)(2,1)S(1)} %shard_map.62.mine), channel_id=1, source_target_pairs={{0,2},{1,3},{2,0},{3,1},{4,6},{5,7},{6,4},{7,5},{8,10},{9,11},{10,... | collective-permute-start | bytes 258056 | tf_op jit(solution)/shard_map/ppermute | solution.py:270
  19.5 1.9 %collective-permute-start.7 = (bf16[48,2560]{1,0:T(8,128)(2,1)S(1)}, bf16[48,2560]{1,0:T(8,128)(2,1)S(1)}, u32[]{:S(2)}, u32[]{:S(2)}) collective-permute-start(bf16[48,2560]{1,0:T(8,128)(2,1)S(1)} %get-tuple-element.18), channel_id=1, source_target_pairs={{0,15},{1,2},{2,1},{3,4},{4,3},{5,6},{6,5},{7,8},{8,7},{9,10},{10,... | collective-permute-start | bytes 737288 | tf_op jit(solution)/shard_map/ppermute | solution.py:270
  21.5 2.5 %collective-permute-start.8 = (bf16[48,2560]{1,0:T(8,128)(2,1)S(1)}, bf16[48,2560]{1,0:T(8,128)(2,1)S(1)}, u32[]{:S(2)}, u32[]{:S(2)}) collective-permute-start(bf16[48,2560]{1,0:T(8,128)(2,1)S(1)} %get-tuple-element.19), channel_id=1, source_target_pairs={{0,15},{1,2},{2,1},{3,4},{4,3},{5,6},{6,5},{7,8},{8,7},{9,10},{10,... | collective-permute-start | bytes 737288 | tf_op jit(solution)/shard_map/ppermute | solution.py:270
  24.0 3.7 %collective-permute-done.3.other = bf16[16,2688]{1,0:T(8,128)(2,1)S(1)} collective-permute-done((bf16[16,2688]{1,0:T(8,128)(2,1)S(1)}, bf16[16,2688]{1,0:T(8,128)(2,1)S(1)}, u32[]{:S(2)}, u32[]{:S(2)}) %collective-permute-start.3) | collective-permute-done | bytes 86048 | tf_op jit(solution)/shard_map/ppermute | solution.py:270
  27.7 0.3 shard_map.63.mine
  28.0 0.6 %collective-permute-start.4 = (bf16[16,2560]{1,0:T(8,128)(2,1)S(1)}, bf16[16,2560]{1,0:T(8,128)(2,1)S(1)}, u32[]{:S(2)}, u32[]{:S(2)}) collective-permute-start(bf16[16,2560]{1,0:T(8,128)(2,1)S(1)} %shard_map.63.mine), channel_id=1, source_target_pairs={{0,4},{1,5},{2,6},{3,7},{4,0},{5,1},{6,2},{7,3},{8,12},{9,13},{10,... | collective-permute-start | bytes 245768 | tf_op jit(solution)/shard_map/ppermute | solution.py:270
  28.6 3.9 %collective-permute-done.4.other = bf16[16,2560]{1,0:T(8,128)(2,1)S(1)} collective-permute-done((bf16[16,2560]{1,0:T(8,128)(2,1)S(1)}, bf16[16,2560]{1,0:T(8,128)(2,1)S(1)}, u32[]{:S(2)}, u32[]{:S(2)}) %collective-permute-start.4) | collective-permute-done | bytes 81952 | tf_op jit(solution)/shard_map/ppermute | solution.py:270
  32.5 0.1 collective-permute-start.5
  32.6 2.9 %shard_map.66.refs_1_ = bf16[2560,1280]{1,0:T(8,128)(2,1)S(1)} custom-call(s32[1]{0:T(128)} %bitcast.place, bf16[2560,2560]{1,0:T(8,128)(2,1)} %source.3), custom_call_target="tpu_custom_call" | custom-call | flops 1 | bytes 13107200 | tf_op jit(solution)/shard_map/pallas_call | solution.py:36
  35.5 0.0 copy-start
  35.5 2.9 %shard_map.65.refs_0_ = bf16[2560,1280]{1,0:T(8,128)(2,1)S(1)} custom-call(s32[1]{0:T(128)} %bitcast.place, bf16[2560,2560]{1,0:T(8,128)(2,1)} %source.3), custom_call_target="tpu_custom_call" | custom-call | flops 1 | bytes 13107200 | tf_op jit(solution)/shard_map/pallas_call | solution.py:36
  38.4 0.0 collective-permute-done.7.refs_0_
  38.4 0.0 collective-permute-done.8.refs_1_
  38.5 0.0 collective-permute-done.6.near
  38.5 0.0 copy-done
  38.5 1.7 %shard_map.67.refs_2_ = bf16[128,2560]{1,0:T(8,128)(2,1)S(1)} custom-call(s32[1]{0:T(128)} %bitcast.place, bf16[128,2560]{1,0:T(8,128)(2,1)S(1)} %bitcast.4, bf16[2,128,2560]{2,1,0:T(8,128)(2,1)S(1)} %get-tuple-element.16.kv, bf16[2,48,2560]{2,1,0:T(8,128)(2,1)S(1)} %collective-permute-done.6.near, bf16[48,2560]{1,0:T(8,128)(2,1)S(1)} %collective-permute-done.7.refs_0_, ...), custom_call_target="tpu_custom_call" | custom-call | flops 335544320 | bytes 3932160 | tf_op jit(solution)/shard_map/pallas_call | solution.py:36
  40.2 0.0 collective-permute-done.5.other
  40.2 3.6 %shard_map.68 = (bf16[128,2560]{1,0:T(8,128)(2,1)}, bf16[64,2560]{1,0:T(8,128)(2,1)}) custom-call(s32[1]{0:T(128)} %bitcast.place, bf16[32,2560]{1,0:T(8,128)(2,1)S(1)} %shard_map.64.mine, bf16[32,2560]{1,0:T(8,128)(2,1)S(1)} %collective-permute-done.5.other, bf16[2560,1280]{1,0:T(8,128)(2,1)S(1)} %shard_map.65.refs_0_, ...), custom_call_target="tpu_custom_call" | custom-call | flops 2516582400 | bytes 13107200 | tf_op jit(solution)/shard_map/pallas_call | solution.py:36
  (1 shorter events, 0.0 us)
Async XLA Ops:
  3.0 1.6 %collective-permute-start = (bf16[32,2688]{1,0:T(8,128)(2,1)S(1)}, bf16[32,2688]{1,0:T(8,128)(2,1)S(1)}, u32[]{:S(2)}, u32[]{:S(2)}) collective-permute-start(bf16[32,2688]{1,0:T(8,128)(2,1)S(1)} %get-tuple-element.13), channel_id=1, source_target_pairs={{0,1},{1,0},{2,3},{3,2},{4,5},{5,4},{6,7},{7,6},{8,9},{9,8},{10,11... | collective-permute-start | bytes 516104 | tf_op jit(solution)/shard_map/ppermute | solution.py:270
  3.6 34.9 %collective-permute-start.6 = (bf16[2,48,2560]{2,1,0:T(8,128)(2,1)S(1)}, bf16[2,48,2560]{2,1,0:T(8,128)(2,1)S(1)}, u32[]{:S(2)}, u32[]{:S(2)}) collective-permute-start(bf16[2,48,2560]{2,1,0:T(8,128)(2,1)S(1)} %get-tuple-element.17), channel_id=1, source_target_pairs={{0,1},{1,0},{2,3},{3,2},{4,5},{5,4},{6,7},{7,6},{8,9},{9,8},{10,11... | collective-permute-start | bytes 1474568 | tf_op jit(solution)/shard_map/ppermute | solution.py:270
  4.9 5.8 %collective-permute-start.1 = (bf16[16,2688]{1,0:T(8,128)(2,1)S(1)}, bf16[16,2688]{1,0:T(8,128)(2,1)S(1)}, u32[]{:S(2)}, u32[]{:S(2)}) collective-permute-start(bf16[16,2688]{1,0:T(8,128)(2,1)S(1)} %get-tuple-element.15), channel_id=1, source_target_pairs={{0,4},{1,5},{2,6},{3,7},{4,0},{5,1},{6,2},{7,3},{8,12},{9,13},{10,... | collective-permute-start | bytes 258056 | tf_op jit(solution)/shard_map/ppermute | solution.py:270
  11.0 6.8 %collective-permute-start.2 = (bf16[16,2688]{1,0:T(8,128)(2,1)S(1)}, bf16[16,2688]{1,0:T(8,128)(2,1)S(1)}, u32[]{:S(2)}, u32[]{:S(2)}) collective-permute-start(bf16[16,2688]{1,0:T(8,128)(2,1)S(1)} %shard_map.61.mine), channel_id=1, source_target_pairs={{0,8},{1,9},{2,10},{3,11},{4,12},{5,13},{6,14},{7,15},{8,0},{9,1},... | collective-permute-start | bytes 258056 | tf_op jit(solution)/shard_map/ppermute | solution.py:270
  18.0 9.7 %collective-permute-start.3 = (bf16[16,2688]{1,0:T(8,128)(2,1)S(1)}, bf16[16,2688]{1,0:T(8,128)(2,1)S(1)}, u32[]{:S(2)}, u32[]{:S(2)}) collective-permute-start(bf16[16,2688]{1,0:T(8,128)(2,1)S(1)} %shard_map.62.mine), channel_id=1, source_target_pairs={{0,2},{1,3},{2,0},{3,1},{4,6},{5,7},{6,4},{7,5},{8,10},{9,11},{10,... | collective-permute-start | bytes 258056 | tf_op jit(solution)/shard_map/ppermute | solution.py:270
  19.5 18.9 %collective-permute-start.7 = (bf16[48,2560]{1,0:T(8,128)(2,1)S(1)}, bf16[48,2560]{1,0:T(8,128)(2,1)S(1)}, u32[]{:S(2)}, u32[]{:S(2)}) collective-permute-start(bf16[48,2560]{1,0:T(8,128)(2,1)S(1)} %get-tuple-element.18), channel_id=1, source_target_pairs={{0,15},{1,2},{2,1},{3,4},{4,3},{5,6},{6,5},{7,8},{8,7},{9,10},{10,... | collective-permute-start | bytes 737288 | tf_op jit(solution)/shard_map/ppermute | solution.py:270
  21.5 17.0 %collective-permute-start.8 = (bf16[48,2560]{1,0:T(8,128)(2,1)S(1)}, bf16[48,2560]{1,0:T(8,128)(2,1)S(1)}, u32[]{:S(2)}, u32[]{:S(2)}) collective-permute-start(bf16[48,2560]{1,0:T(8,128)(2,1)S(1)} %get-tuple-element.19), channel_id=1, source_target_pairs={{0,15},{1,2},{2,1},{3,4},{4,3},{5,6},{6,5},{7,8},{8,7},{9,10},{10,... | collective-permute-start | bytes 737288 | tf_op jit(solution)/shard_map/ppermute | solution.py:270
  28.0 4.5 %collective-permute-start.4 = (bf16[16,2560]{1,0:T(8,128)(2,1)S(1)}, bf16[16,2560]{1,0:T(8,128)(2,1)S(1)}, u32[]{:S(2)}, u32[]{:S(2)}) collective-permute-start(bf16[16,2560]{1,0:T(8,128)(2,1)S(1)} %shard_map.63.mine), channel_id=1, source_target_pairs={{0,4},{1,5},{2,6},{3,7},{4,0},{5,1},{6,2},{7,3},{8,12},{9,13},{10,... | collective-permute-start | bytes 245768 | tf_op jit(solution)/shard_map/ppermute | solution.py:270
  32.5 7.7 %collective-permute-start.5 = (bf16[32,2560]{1,0:T(8,128)(2,1)S(1)}, bf16[32,2560]{1,0:T(8,128)(2,1)S(1)}, u32[]{:S(2)}, u32[]{:S(2)}) collective-permute-start(bf16[32,2560]{1,0:T(8,128)(2,1)S(1)} %shard_map.64.mine), channel_id=1, source_target_pairs={{0,1},{1,0},{2,3},{3,2},{4,5},{5,4},{6,7},{7,6},{8,9},{9,8},{10,11... | collective-permute-start | bytes 491528 | tf_op jit(solution)/shard_map/ppermute | solution.py:270
  35.5 3.0 %copy-start = (bf16[16,8,2560]{2,1,0:T(8,128)(2,1)S(1)}, bf16[16,8,2560]{2,1,0:T(8,128)(2,1)}, u32[]{:S(2)}) copy-start(bf16[16,8,2560]{2,1,0:T(8,128)(2,1)} %param.4) | copy-start | bytes 1966084

commit v2 on v1

--- a/solution.py
+++ b/solution.py
@@ -16,11 +16,12 @@
 SCALE = math.log2(math.e) / math.sqrt(HEAD_DIM)
 NEG = -1e30
 GROUP = 32
-CHUNKS = 1
+CHUNKS = 4
 BATCH = 10
 ABATCH = 5
 PIECES = 2
-LOADS = 2
+LOADS = ()
+COUNT = max(1, len(LOADS))
 MIB = 1 << 20
 
 
@@ -65,9 +66,8 @@
         far[piece][:, at : at + HEAD_DIM] = value[:, low : low + HEAD_DIM]
 
 
-def first_body(cols, place, kv_hbm, r_hbm, kv, near, keep, send, *refs):
-    far, (r, sems) = refs[:-2], refs[-2:]
-    tokens, width = kv_hbm.shape[1:]
+def first_body(place, kv_hbm, r_hbm, kv, keep, send, r, sems):
+    _, width = kv_hbm.shape[1:]
     rows = r_hbm.shape[0]
     half = rows // 2
     steps = HEADS // BATCH
@@ -84,13 +84,6 @@
     for copy in copies:
         copy.start()
     bit = place[0] % 2
-    count = tokens // cols * RADIUS
-    row, token = iota((count, tokens), 0), iota((count, tokens), 1)
-    base = row // RADIUS * cols + row % RADIUS
-    high = cols - RADIUS
-    pick_near = (token == base + jnp.where(bit == 1, 0, high)).astype(jnp.bfloat16)
-    pick_far = (token == base + jnp.where(bit == 1, high, 0)).astype(jnp.bfloat16)
-    pick = jnp.concatenate([pick_near, pick_far], axis=0)
     lane = iota((rows, HEAD_DIM), 1)
     peaks = jnp.zeros((rows, HEAD_DIM), jnp.float32)
     totals = jnp.zeros((rows, HEAD_DIM), jnp.float32)
@@ -106,11 +99,6 @@
         heads = range(step * BATCH, (step + 1) * BATCH)
         at = [slice(head * HEAD_DIM, (head + 1) * HEAD_DIM) for head in heads]
         scores = [mm(r[:, x], kv[0, :, x], ((1,), (1,))) * SCALE for x in at]
-        whole = slice(step * block, (step + 1) * block)
-        for part in range(2):
-            picked = mm(pick, kv[part, :, whole]).astype(jnp.bfloat16)
-            near[part, :, whole] = picked[:count]
-            spread(far, part, step * block, picked[count:])
         tops = [jnp.max(x, axis=-1, keepdims=True) for x in scores]
         tops = [x.astype(jnp.bfloat16).astype(jnp.float32) for x in tops]
         weights = [jnp.exp2(x - top) for x, top in zip(scores, tops)]
@@ -123,6 +111,25 @@
     rounded = totals.astype(jnp.bfloat16).astype(jnp.float32)
     stats = jnp.where(lane < GROUP, peaks, jnp.where(lane < 2 * GROUP, rounded, totals - rounded))
     store(stats, slice(width, width + HEAD_DIM))
+
+
+def pack_body(cols, place, kv, near, *far):
+    tokens, width = kv.shape[1:]
+    bit = place[0] % 2
+    count = tokens // cols * RADIUS
+    row, token = iota((count, tokens), 0), iota((count, tokens), 1)
+    base = row // RADIUS * cols + row % RADIUS
+    high = cols - RADIUS
+    pick_near = (token == base + jnp.where(bit == 1, 0, high)).astype(jnp.bfloat16)
+    pick_far = (token == base + jnp.where(bit == 1, high, 0)).astype(jnp.bfloat16)
+    pick = jnp.concatenate([pick_near, pick_far], axis=0)
+    block = 512
+    for start in range(0, width, block):
+        whole = slice(start, start + block)
+        for part in range(2):
+            picked = mm(pick, kv[part, :, whole]).astype(jnp.bfloat16)
+            near[part, :, whole] = picked[:count]
+            spread(far, part, start, picked[count:])
 
 
 def merge_body(level, split, last, place, mine, other, *outs):
@@ -223,15 +230,15 @@
     join(out, 0, (place[0] // level) % 2, mine, other)
 
 
-def load_body(part, place, source, target, sem):
+def load_body(start, place, source, target, sem):
     columns = target.shape[1]
-    copy = pltpu.make_async_copy(source.at[:, pl.ds(part * columns, columns)], target, sem)
+    copy = pltpu.make_async_copy(source.at[:, pl.ds(start, columns)], target, sem)
     copy.start()
     copy.wait()
 
 
 def project_body(place, mine, other, *refs):
-    weights, blended = refs[:LOADS], refs[LOADS:-4]
+    weights, blended = refs[:COUNT], refs[COUNT:-4]
     (out, reg_out), (x, projected) = refs[-4:-2], refs[-2:]
     tokens = out.shape[0]
     width = out.shape[1]
@@ -240,16 +247,17 @@
         x[:tokens, start : start + piece.shape[1]] = piece[...]
         start += piece.shape[1]
     join(x, tokens, place[0] % 2, mine, other)
-    span = weights[0].shape[1]
-    block = math.gcd(span, 512)
+    block = 512
+    start = 0
     square = jnp.zeros((reg_out.shape[0], 1), jnp.float32)
-    for start in range(0, width, block):
-        low = start % span
-        y = mm(x[...], weights[start // span][:, low : low + block])
-        out[:, start : start + block] = y[:tokens].astype(jnp.bfloat16)
-        r = y[tokens:]
-        projected[:, start : start + block] = r
-        square = square + jnp.sum(r * r, axis=-1, keepdims=True)
+    for weight in weights:
+        for low in range(0, weight.shape[1], block):
+            y = mm(x[...], weight[:, low : low + block])
+            out[:, start : start + block] = y[:tokens].astype(jnp.bfloat16)
+            r = y[tokens:]
+            projected[:, start : start + block] = r
+            square = square + jnp.sum(r * r, axis=-1, keepdims=True)
+            start += block
     scale = lax.rsqrt(square / width + 1e-06)
     reg_out[...] = (projected[...] * scale).astype(jnp.bfloat16)
 
@@ -276,12 +284,10 @@
 
     wide = model_width + HEAD_DIM
     hbm = [pltpu.with_memory_space_constraint(x, pltpu.HBM) for x in (kv, reg_queries)]
-    kv, near, keep, send, *far = call(
-        functools.partial(first_body, columns),
-        [(kv.shape, bf16), ((2, edge, model_width), bf16)]
-        + [((regs // 2, wide), jnp.float32), ((regs // 2, wide), bf16)]
-        + [((edge, 2 * model_width // PIECES), bf16)] * PIECES,
-        flops=8 * edge * tokens * model_width + 4 * regs * tokens * model_width,
+    kv, keep, send = call(
+        first_body,
+        [(kv.shape, bf16), ((regs // 2, wide), jnp.float32), ((regs // 2, wide), bf16)],
+        flops=4 * regs * tokens * model_width,
         moved=kv.size * 2,
         exps=regs * tokens * HEADS,
         scratch=(
@@ -290,6 +296,12 @@
         ),
         space=HBM,
     )(place, *hbm)
+    near, *far = call(
+        functools.partial(pack_body, columns),
+        [((2, edge, model_width), bf16)] + [((edge, 2 * model_width // PIECES), bf16)] * PIECES,
+        flops=8 * edge * tokens * model_width,
+        moved=kv.size * 2,
+    )(place, kv)
     far_in = []
     for piece in range(PIECES):
         far_in.append(exchange(far[piece], pairs_far))
@@ -300,8 +312,6 @@
     while level < size:
         levels.append(level)
         level *= 2
-    if len(levels) > 2:
-        levels.append(levels.pop(1))
     halved = min(2, len(levels) - 1)
     other = exchange(send, flip(1))
     for step, level in enumerate(levels):
@@ -343,13 +353,13 @@
         blended.append(piece)
 
     weight_hbm = pltpu.with_memory_space_constraint(out_weight, pltpu.HBM)
-    weights = []
-    for part in range(LOADS):
+    weights = [] if LOADS else [out_weight]
+    for part, columns_here in enumerate(LOADS):
         weights += call(
-            functools.partial(load_body, part),
-            [((model_width, model_width // LOADS), bf16)],
+            functools.partial(load_body, sum(LOADS[:part])),
+            [((model_width, columns_here), bf16)],
             flops=1,
-            moved=4 * model_width * model_width // LOADS,
+            moved=4 * model_width * columns_here,
             scratch=(pltpu.SemaphoreType.DMA,),
             space=HBM,
         )(place, weight_hbm)

time: 44.2 us -> 40.2 us (0.910)
  Pallas kernels: 14.5 us -> 9.69 us
  waiting for transfers between devices: 15.4 us -> 16.6 us
    pallas_call x10 -> x12, Pallas kernels: 14.5 us -> 9.69 us  [run(): pl.pallas_call(body, out_shape=shapes, in_specs=[SMEM] + [space] * (len(a...]
    ppermute x9, waiting for transfers between devices: 15.4 us -> 16.6 us  [exchange(): return lax.ppermute(x, 'lon', pairs)]
  transfers between devices with their start and end apart: 9 -> 9, of which waited for: 5 -> 4; matrix products, arithmetic and copies ran while one was open for 0% -> 0% of each run, Pallas kernels for 19% -> 9%
where the time goes in v2:
time: 40.2 us; the launch traced here: 40 us
  waiting for transfers between devices  16.6 us (41%)
  starting transfers between devices  12.9 us (32%)
  Pallas kernels  9.69 us (24%)
  between operations  0.78 us (2%)
    ppermute x9, waiting for transfers between devices, exchange(): return lax.ppermute(x, 'lon', pairs)  16.6 us
    ppermute x9, starting transfers between devices, exchange(): return lax.ppermute(x, 'lon', pairs)  12.9 us
    pallas_call x12, Pallas kernels, run(): pl.pallas_call(body, out_shape=shapes, in_specs=[SMEM] + [space] * (len(a...  9.69 us
  transfers between devices with their start and end apart: 9, of which 4 were waited for; matrix products, arithmetic and copies ran while one was open for 0% of the time, Pallas kernels for 9%

profile of v2, /device:TPU:0, one launch (start us, length us, event | category | flops | bytes accessed | tf_op | source)
XLA Modules:
  0.0 40.0 jit_solution(72983440077807852)
XLA Ops:
  0.6 2.3 %shard_map.59 = (bf16[2,128,2560]{2,1,0:T(8,128)(2,1)S(1)}, f32[32,2688]{1,0:T(8,128)S(1)}, bf16[32,2688]{1,0:T(8,128)(2,1)S(1)}) custom-call(s32[1]{0:T(128)} %bitcast.place, bf16[2,128,2560]{2,1,0:T(8,128)(2,1)} %bitcast.8, bf16[64,2560]{1,0:T(8,128)(2,1)} %r_hbm.1), custom_call_target="tpu_custom_call" | custom-call | flops 83886080 | bytes 1310720 | tf_op jit(solution)/shard_map/pallas_call | solution.py:37
  3.0 0.6 %collective-permute-start = (bf16[32,2688]{1,0:T(8,128)(2,1)S(1)}, bf16[32,2688]{1,0:T(8,128)(2,1)S(1)}, u32[]{:S(2)}, u32[]{:S(2)}) collective-permute-start(bf16[32,2688]{1,0:T(8,128)(2,1)S(1)} %get-tuple-element.13), channel_id=1, source_target_pairs={{0,1},{1,0},{2,3},{3,2},{4,5},{5,4},{6,7},{7,6},{8,9},{9,8},{10,11... | collective-permute-start | bytes 516104 | tf_op jit(solution)/shard_map/ppermute | solution.py:278
  3.5 0.0 copy-start.1
  3.5 0.4 %shard_map.65 = (bf16[2,48,2560]{2,1,0:T(8,128)(2,1)S(1)}, bf16[48,2560]{1,0:T(8,128)(2,1)S(1)}, bf16[48,2560]{1,0:T(8,128)(2,1)S(1)}) custom-call(s32[1]{0:T(128)} %bitcast.place, bf16[2,128,2560]{2,1,0:T(8,128)(2,1)S(1)} %get-tuple-element.16.kv), custom_call_target="tpu_custom_call" | custom-call | flops 125829120 | bytes 1310720 | tf_op jit(solution)/shard_map/pallas_call | solution.py:37
  4.0 0.1 collective-permute-start.6
  4.1 0.5 %collective-permute-done.other = bf16[32,2688]{1,0:T(8,128)(2,1)S(1)} collective-permute-done((bf16[32,2688]{1,0:T(8,128)(2,1)S(1)}, bf16[32,2688]{1,0:T(8,128)(2,1)S(1)}, u32[]{:S(2)}, u32[]{:S(2)}) %collective-permute-start) | collective-permute-done | bytes 172064 | tf_op jit(solution)/shard_map/ppermute | solution.py:278
  4.6 0.3 shard_map.60
  4.9 2.9 %collective-permute-start.1 = (bf16[16,2688]{1,0:T(8,128)(2,1)S(1)}, bf16[16,2688]{1,0:T(8,128)(2,1)S(1)}, u32[]{:S(2)}, u32[]{:S(2)}) collective-permute-start(bf16[16,2688]{1,0:T(8,128)(2,1)S(1)} %get-tuple-element.15), channel_id=1, source_target_pairs={{0,2},{1,3},{2,0},{3,1},{4,6},{5,7},{6,4},{7,5},{8,10},{9,11},{10,... | collective-permute-start | bytes 258056 | tf_op jit(solution)/shard_map/ppermute | solution.py:278
  7.8 2.8 %collective-permute-done.1.other = bf16[16,2688]{1,0:T(8,128)(2,1)S(1)} collective-permute-done((bf16[16,2688]{1,0:T(8,128)(2,1)S(1)}, bf16[16,2688]{1,0:T(8,128)(2,1)S(1)}, u32[]{:S(2)}, u32[]{:S(2)}) %collective-permute-start.1) | collective-permute-done | bytes 86048 | tf_op jit(solution)/shard_map/ppermute | solution.py:278
  10.7 0.2 shard_map.61.mine
  10.9 1.9 %collective-permute-start.2 = (bf16[16,2688]{1,0:T(8,128)(2,1)S(1)}, bf16[16,2688]{1,0:T(8,128)(2,1)S(1)}, u32[]{:S(2)}, u32[]{:S(2)}) collective-permute-start(bf16[16,2688]{1,0:T(8,128)(2,1)S(1)} %shard_map.61.mine), channel_id=1, source_target_pairs={{0,4},{1,5},{2,6},{3,7},{4,0},{5,1},{6,2},{7,3},{8,12},{9,13},{10,... | collective-permute-start | bytes 258056 | tf_op jit(solution)/shard_map/ppermute | solution.py:278
  12.7 2.7 %collective-permute-done.2.other = bf16[16,2688]{1,0:T(8,128)(2,1)S(1)} collective-permute-done((bf16[16,2688]{1,0:T(8,128)(2,1)S(1)}, bf16[16,2688]{1,0:T(8,128)(2,1)S(1)}, u32[]{:S(2)}, u32[]{:S(2)}) %collective-permute-start.2) | collective-permute-done | bytes 86048 | tf_op jit(solution)/shard_map/ppermute | solution.py:278
  15.4 0.0 copy-start
  15.4 0.2 shard_map.62.mine
  15.6 2.9 %collective-permute-start.3 = (bf16[16,2688]{1,0:T(8,128)(2,1)S(1)}, bf16[16,2688]{1,0:T(8,128)(2,1)S(1)}, u32[]{:S(2)}, u32[]{:S(2)}) collective-permute-start(bf16[16,2688]{1,0:T(8,128)(2,1)S(1)} %shard_map.62.mine), channel_id=1, source_target_pairs={{0,8},{1,9},{2,10},{3,11},{4,12},{5,13},{6,14},{7,15},{8,0},{9,1},... | collective-permute-start | bytes 258056 | tf_op jit(solution)/shard_map/ppermute | solution.py:278
  18.5 0.0 collective-permute-start.7
  18.5 4.4 %collective-permute-start.8 = (bf16[48,2560]{1,0:T(8,128)(2,1)S(1)}, bf16[48,2560]{1,0:T(8,128)(2,1)S(1)}, u32[]{:S(2)}, u32[]{:S(2)}) collective-permute-start(bf16[48,2560]{1,0:T(8,128)(2,1)S(1)} %get-tuple-element.19), channel_id=1, source_target_pairs={{0,15},{1,2},{2,1},{3,4},{4,3},{5,6},{6,5},{7,8},{8,7},{9,10},{10,... | collective-permute-start | bytes 737288 | tf_op jit(solution)/shard_map/ppermute | solution.py:278
  22.9 0.0 collective-permute-done.3.other
  22.9 0.3 shard_map.63.mine
  23.2 0.1 collective-permute-start.4
  23.3 10.6 %collective-permute-done.4.other = bf16[16,2560]{1,0:T(8,128)(2,1)S(1)} collective-permute-done((bf16[16,2560]{1,0:T(8,128)(2,1)S(1)}, bf16[16,2560]{1,0:T(8,128)(2,1)S(1)}, u32[]{:S(2)}, u32[]{:S(2)}) %collective-permute-start.4) | collective-permute-done | bytes 81952 | tf_op jit(solution)/shard_map/ppermute | solution.py:278
  33.9 0.1 collective-permute-start.5
  33.9 0.0 collective-permute-done.7.refs_0_
  34.0 0.0 collective-permute-done.8.refs_1_
  34.0 0.0 collective-permute-done.6.near
  34.0 0.0 copy-done.1
  34.0 0.6 %shard_map.69.refs_4_ = bf16[128,640]{1,0:T(8,128)(2,1)S(1)} custom-call(s32[1]{0:T(128)} %bitcast.place, bf16[128,2560]{1,0:T(8,128)(2,1)S(1)} %bitcast.4, bf16[2,128,2560]{2,1,0:T(8,128)(2,1)S(1)} %get-tuple-element.16.kv, bf16[2,48,2560]{2,1,0:T(8,128)(2,1)S(1)} %collective-permute-done.6.near, bf16[48,2560]{1,0:T(8,128)(2,1)S(1)} %collective-permute-done.7.refs_0_, ...), custom_call_target="tpu_custom_call" | custom-call | flops 83886080 | bytes 983040 | tf_op jit(solution)/shard_map/pallas_call | solution.py:37
  34.6 0.6 %shard_map.68.refs_3_ = bf16[128,640]{1,0:T(8,128)(2,1)S(1)} custom-call(s32[1]{0:T(128)} %bitcast.place, bf16[128,2560]{1,0:T(8,128)(2,1)S(1)} %bitcast.5, bf16[2,128,2560]{2,1,0:T(8,128)(2,1)S(1)} %get-tuple-element.16.kv, bf16[2,48,2560]{2,1,0:T(8,128)(2,1)S(1)} %collective-permute-done.6.near, bf16[48,2560]{1,0:T(8,128)(2,1)S(1)} %collective-permute-done.7.refs_0_, ...), custom_call_target="tpu_custom_call" | custom-call | flops 83886080 | bytes 983040 | tf_op jit(solution)/shard_map/pallas_call | solution.py:37
  35.2 0.6 %shard_map.67.refs_2_ = bf16[128,640]{1,0:T(8,128)(2,1)S(1)} custom-call(s32[1]{0:T(128)} %bitcast.place, bf16[128,2560]{1,0:T(8,128)(2,1)S(1)} %bitcast.6, bf16[2,128,2560]{2,1,0:T(8,128)(2,1)S(1)} %get-tuple-element.16.kv, bf16[2,48,2560]{2,1,0:T(8,128)(2,1)S(1)} %collective-permute-done.6.near, bf16[48,2560]{1,0:T(8,128)(2,1)S(1)} %collective-permute-done.7.refs_0_, ...), custom_call_target="tpu_custom_call" | custom-call | flops 83886080 | bytes 983040 | tf_op jit(solution)/shard_map/pallas_call | solution.py:37
  35.8 0.6 %shard_map.66.refs_1_ = bf16[128,640]{1,0:T(8,128)(2,1)S(1)} custom-call(s32[1]{0:T(128)} %bitcast.place, bf16[128,2560]{1,0:T(8,128)(2,1)S(1)} %bitcast.7, bf16[2,128,2560]{2,1,0:T(8,128)(2,1)S(1)} %get-tuple-element.16.kv, bf16[2,48,2560]{2,1,0:T(8,128)(2,1)S(1)} %collective-permute-done.6.near, bf16[48,2560]{1,0:T(8,128)(2,1)S(1)} %collective-permute-done.7.refs_0_, ...), custom_call_target="tpu_custom_call" | custom-call | flops 83886080 | bytes 983040 | tf_op jit(solution)/shard_map/pallas_call | solution.py:37
  36.3 0.0 collective-permute-done.5.other
  36.4 0.0 copy-done
  36.4 3.7 %shard_map.70 = (bf16[128,2560]{1,0:T(8,128)(2,1)}, bf16[64,2560]{1,0:T(8,128)(2,1)}) custom-call(s32[1]{0:T(128)} %bitcast.place, bf16[32,2560]{1,0:T(8,128)(2,1)S(1)} %shard_map.64.mine, bf16[32,2560]{1,0:T(8,128)(2,1)S(1)} %collective-permute-done.5.other, bf16[2560,2560]{1,0:T(8,128)(2,1)S(1)} %copy-done, bf16[128,640]{1,0:T(8,128)(2,1)S(1)} %shard_map.66.refs_1_, ...), custom_call_target="tpu_custom_call" | custom-call | flops 2516582400 | bytes 13107200 | tf_op jit(solution)/shard_map/pallas_call | solution.py:37
  (1 shorter events, 0.0 us)
Async XLA Ops:
  3.0 1.6 %collective-permute-start = (bf16[32,2688]{1,0:T(8,128)(2,1)S(1)}, bf16[32,2688]{1,0:T(8,128)(2,1)S(1)}, u32[]{:S(2)}, u32[]{:S(2)}) collective-permute-start(bf16[32,2688]{1,0:T(8,128)(2,1)S(1)} %get-tuple-element.13), channel_id=1, source_target_pairs={{0,1},{1,0},{2,3},{3,2},{4,5},{5,4},{6,7},{7,6},{8,9},{9,8},{10,11... | collective-permute-start | bytes 516104 | tf_op jit(solution)/shard_map/ppermute | solution.py:278
  3.5 30.4 %copy-start.1 = (bf16[16,8,2560]{2,1,0:T(8,128)(2,1)S(1)}, bf16[16,8,2560]{2,1,0:T(8,128)(2,1)}, u32[]{:S(2)}) copy-start(bf16[16,8,2560]{2,1,0:T(8,128)(2,1)} %param.4) | copy-start | bytes 1966084
  4.0 30.0 %collective-permute-start.6 = (bf16[2,48,2560]{2,1,0:T(8,128)(2,1)S(1)}, bf16[2,48,2560]{2,1,0:T(8,128)(2,1)S(1)}, u32[]{:S(2)}, u32[]{:S(2)}) collective-permute-start(bf16[2,48,2560]{2,1,0:T(8,128)(2,1)S(1)} %get-tuple-element.17), channel_id=1, source_target_pairs={{0,1},{1,0},{2,3},{3,2},{4,5},{5,4},{6,7},{7,6},{8,9},{9,8},{10,11... | collective-permute-start | bytes 1474568 | tf_op jit(solution)/shard_map/ppermute | solution.py:278
  4.9 5.8 %collective-permute-start.1 = (bf16[16,2688]{1,0:T(8,128)(2,1)S(1)}, bf16[16,2688]{1,0:T(8,128)(2,1)S(1)}, u32[]{:S(2)}, u32[]{:S(2)}) collective-permute-start(bf16[16,2688]{1,0:T(8,128)(2,1)S(1)} %get-tuple-element.15), channel_id=1, source_target_pairs={{0,2},{1,3},{2,0},{3,1},{4,6},{5,7},{6,4},{7,5},{8,10},{9,11},{10,... | collective-permute-start | bytes 258056 | tf_op jit(solution)/shard_map/ppermute | solution.py:278
  10.9 4.6 %collective-permute-start.2 = (bf16[16,2688]{1,0:T(8,128)(2,1)S(1)}, bf16[16,2688]{1,0:T(8,128)(2,1)S(1)}, u32[]{:S(2)}, u32[]{:S(2)}) collective-permute-start(bf16[16,2688]{1,0:T(8,128)(2,1)S(1)} %shard_map.61.mine), channel_id=1, source_target_pairs={{0,4},{1,5},{2,6},{3,7},{4,0},{5,1},{6,2},{7,3},{8,12},{9,13},{10,... | collective-permute-start | bytes 258056 | tf_op jit(solution)/shard_map/ppermute | solution.py:278
  15.4 20.9 %copy-start = (bf16[2560,2560]{1,0:T(8,128)(2,1)S(1)}, bf16[2560,2560]{1,0:T(8,128)(2,1)}, u32[]{:S(2)}) copy-start(bf16[2560,2560]{1,0:T(8,128)(2,1)} %refs_0_.1) | copy-start | bytes 39321604
  15.6 7.3 %collective-permute-start.3 = (bf16[16,2688]{1,0:T(8,128)(2,1)S(1)}, bf16[16,2688]{1,0:T(8,128)(2,1)S(1)}, u32[]{:S(2)}, u32[]{:S(2)}) collective-permute-start(bf16[16,2688]{1,0:T(8,128)(2,1)S(1)} %shard_map.62.mine), channel_id=1, source_target_pairs={{0,8},{1,9},{2,10},{3,11},{4,12},{5,13},{6,14},{7,15},{8,0},{9,1},... | collective-permute-start | bytes 258056 | tf_op jit(solution)/shard_map/ppermute | solution.py:278
  18.5 15.5 %collective-permute-start.7 = (bf16[48,2560]{1,0:T(8,128)(2,1)S(1)}, bf16[48,2560]{1,0:T(8,128)(2,1)S(1)}, u32[]{:S(2)}, u32[]{:S(2)}) collective-permute-start(bf16[48,2560]{1,0:T(8,128)(2,1)S(1)} %get-tuple-element.18), channel_id=1, source_target_pairs={{0,15},{1,2},{2,1},{3,4},{4,3},{5,6},{6,5},{7,8},{8,7},{9,10},{10,... | collective-permute-start | bytes 737288 | tf_op jit(solution)/shard_map/ppermute | solution.py:278
  18.5 15.5 %collective-permute-start.8 = (bf16[48,2560]{1,0:T(8,128)(2,1)S(1)}, bf16[48,2560]{1,0:T(8,128)(2,1)S(1)}, u32[]{:S(2)}, u32[]{:S(2)}) collective-permute-start(bf16[48,2560]{1,0:T(8,128)(2,1)S(1)} %get-tuple-element.19), channel_id=1, source_target_pairs={{0,15},{1,2},{2,1},{3,4},{4,3},{5,6},{6,5},{7,8},{8,7},{9,10},{10,... | collective-permute-start | bytes 737288 | tf_op jit(solution)/shard_map/ppermute | solution.py:278
  23.2 10.6 %collective-permute-start.4 = (bf16[16,2560]{1,0:T(8,128)(2,1)S(1)}, bf16[16,2560]{1,0:T(8,128)(2,1)S(1)}, u32[]{:S(2)}, u32[]{:S(2)}) collective-permute-start(bf16[16,2560]{1,0:T(8,128)(2,1)S(1)} %shard_map.63.mine), channel_id=1, source_target_pairs={{0,2},{1,3},{2,0},{3,1},{4,6},{5,7},{6,4},{7,5},{8,10},{9,11},{10,... | collective-permute-start | bytes 245768 | tf_op jit(solution)/shard_map/ppermute | solution.py:278
  33.9 2.5 %collective-permute-start.5 = (bf16[32,2560]{1,0:T(8,128)(2,1)S(1)}, bf16[32,2560]{1,0:T(8,128)(2,1)S(1)}, u32[]{:S(2)}, u32[]{:S(2)}) collective-permute-start(bf16[32,2560]{1,0:T(8,128)(2,1)S(1)} %shard_map.64.mine), channel_id=1, source_target_pairs={{0,1},{1,0},{2,3},{3,2},{4,5},{5,4},{6,7},{7,6},{8,9},{9,8},{10,11... | collective-permute-start | bytes 491528 | tf_op jit(solution)/shard_map/ppermute | solution.py:278

commit v3 on v2

--- a/solution.py
+++ b/solution.py
@@ -17,7 +17,7 @@
 NEG = -1e30
 GROUP = 32
 CHUNKS = 4
-BATCH = 10
+BATCH = HEADS
 ABATCH = 5
 PIECES = 2
 LOADS = ()
@@ -72,13 +72,14 @@
     half = rows // 2
     steps = HEADS // BATCH
     block = BATCH * HEAD_DIM
-    copies = [pltpu.make_async_copy(r_hbm, r, sems.at[steps])]
+    copies = [pltpu.make_async_copy(r_hbm, r, sems.at[2 * steps])]
     copies += [
         pltpu.make_async_copy(
-            kv_hbm.at[:, :, pl.ds(step * block, block)],
-            kv.at[:, :, pl.ds(step * block, block)],
-            sems.at[step],
+            kv_hbm.at[part, :, pl.ds(step * block, block)],
+            kv.at[part, :, pl.ds(step * block, block)],
+            sems.at[part * steps + step],
         )
+        for part in range(2)
         for step in range(steps)
     ]
     for copy in copies:
@@ -99,6 +100,7 @@
         heads = range(step * BATCH, (step + 1) * BATCH)
         at = [slice(head * HEAD_DIM, (head + 1) * HEAD_DIM) for head in heads]
         scores = [mm(r[:, x], kv[0, :, x], ((1,), (1,))) * SCALE for x in at]
+        copies[steps + step + 1].wait()
         tops = [jnp.max(x, axis=-1, keepdims=True) for x in scores]
         tops = [x.astype(jnp.bfloat16).astype(jnp.float32) for x in tops]
         weights = [jnp.exp2(x - top) for x, top in zip(scores, tops)]
@@ -123,7 +125,7 @@
     pick_near = (token == base + jnp.where(bit == 1, 0, high)).astype(jnp.bfloat16)
     pick_far = (token == base + jnp.where(bit == 1, high, 0)).astype(jnp.bfloat16)
     pick = jnp.concatenate([pick_near, pick_far], axis=0)
-    block = 512
+    block = 1280
     for start in range(0, width, block):
         whole = slice(start, start + block)
         for part in range(2):
@@ -247,7 +249,7 @@
         x[:tokens, start : start + piece.shape[1]] = piece[...]
         start += piece.shape[1]
     join(x, tokens, place[0] % 2, mine, other)
-    block = 512
+    block = 256
     start = 0
     square = jnp.zeros((reg_out.shape[0], 1), jnp.float32)
     for weight in weights:
@@ -292,7 +294,7 @@
         exps=regs * tokens * HEADS,
         scratch=(
             pltpu.VMEM(reg_queries.shape, bf16),
-            pltpu.SemaphoreType.DMA((HEADS // BATCH + 1,)),
+            pltpu.SemaphoreType.DMA((2 * (HEADS // BATCH) + 1,)),
         ),
         space=HBM,
     )(place, *hbm)

time: 40.2 us -> 40 us (level)
  no operation moved by 1% of the time
where the time goes in v3:
time: 40 us; the launch traced here: 39.9 us
  waiting for transfers between devices  16.6 us (42%)
  starting transfers between devices  12.9 us (32%)
  Pallas kernels  9.57 us (24%)
  between operations  0.78 us (2%)
    ppermute x9, waiting for transfers between devices, exchange(): return lax.ppermute(x, 'lon', pairs)  16.6 us
    ppermute x9, starting transfers between devices, exchange(): return lax.ppermute(x, 'lon', pairs)  12.9 us
    pallas_call x12, Pallas kernels, run(): pl.pallas_call(body, out_shape=shapes, in_specs=[SMEM] + [space] * (len(a...  9.57 us
  transfers between devices with their start and end apart: 9, of which 4 were waited for; matrix products, arithmetic and copies ran while one was open for 0% of the time, Pallas kernels for 9%

profile of v3, /device:TPU:0, one launch (start us, length us, event | category | flops | bytes accessed | tf_op | source)
XLA Modules:
  0.0 39.9 jit_solution(13358029886465428170)
XLA Ops:
  0.6 2.2 %shard_map.59 = (bf16[2,128,2560]{2,1,0:T(8,128)(2,1)S(1)}, f32[32,2688]{1,0:T(8,128)S(1)}, bf16[32,2688]{1,0:T(8,128)(2,1)S(1)}) custom-call(s32[1]{0:T(128)} %bitcast.place, bf16[2,128,2560]{2,1,0:T(8,128)(2,1)} %bitcast.8, bf16[64,2560]{1,0:T(8,128)(2,1)} %r_hbm.1), custom_call_target="tpu_custom_call" | custom-call | flops 83886080 | bytes 1310720 | tf_op jit(solution)/shard_map/pallas_call | solution.py:37
  2.9 0.6 %collective-permute-start = (bf16[32,2688]{1,0:T(8,128)(2,1)S(1)}, bf16[32,2688]{1,0:T(8,128)(2,1)S(1)}, u32[]{:S(2)}, u32[]{:S(2)}) collective-permute-start(bf16[32,2688]{1,0:T(8,128)(2,1)S(1)} %get-tuple-element.13), channel_id=1, source_target_pairs={{0,1},{1,0},{2,3},{3,2},{4,5},{5,4},{6,7},{7,6},{8,9},{9,8},{10,11... | collective-permute-start | bytes 516104 | tf_op jit(solution)/shard_map/ppermute | solution.py:280
  3.4 0.0 copy-start.1
  3.4 0.4 %shard_map.65 = (bf16[2,48,2560]{2,1,0:T(8,128)(2,1)S(1)}, bf16[48,2560]{1,0:T(8,128)(2,1)S(1)}, bf16[48,2560]{1,0:T(8,128)(2,1)S(1)}) custom-call(s32[1]{0:T(128)} %bitcast.place, bf16[2,128,2560]{2,1,0:T(8,128)(2,1)S(1)} %get-tuple-element.16.kv), custom_call_target="tpu_custom_call" | custom-call | flops 125829120 | bytes 1310720 | tf_op jit(solution)/shard_map/pallas_call | solution.py:37
  3.8 0.1 collective-permute-start.6
  3.9 0.5 %collective-permute-done.other = bf16[32,2688]{1,0:T(8,128)(2,1)S(1)} collective-permute-done((bf16[32,2688]{1,0:T(8,128)(2,1)S(1)}, bf16[32,2688]{1,0:T(8,128)(2,1)S(1)}, u32[]{:S(2)}, u32[]{:S(2)}) %collective-permute-start) | collective-permute-done | bytes 172064 | tf_op jit(solution)/shard_map/ppermute | solution.py:280
  4.5 0.3 shard_map.60
  4.8 2.9 %collective-permute-start.1 = (bf16[16,2688]{1,0:T(8,128)(2,1)S(1)}, bf16[16,2688]{1,0:T(8,128)(2,1)S(1)}, u32[]{:S(2)}, u32[]{:S(2)}) collective-permute-start(bf16[16,2688]{1,0:T(8,128)(2,1)S(1)} %get-tuple-element.15), channel_id=1, source_target_pairs={{0,2},{1,3},{2,0},{3,1},{4,6},{5,7},{6,4},{7,5},{8,10},{9,11},{10,... | collective-permute-start | bytes 258056 | tf_op jit(solution)/shard_map/ppermute | solution.py:280
  7.7 2.8 %collective-permute-done.1.other = bf16[16,2688]{1,0:T(8,128)(2,1)S(1)} collective-permute-done((bf16[16,2688]{1,0:T(8,128)(2,1)S(1)}, bf16[16,2688]{1,0:T(8,128)(2,1)S(1)}, u32[]{:S(2)}, u32[]{:S(2)}) %collective-permute-start.1) | collective-permute-done | bytes 86048 | tf_op jit(solution)/shard_map/ppermute | solution.py:280
  10.5 0.2 shard_map.61.mine
  10.7 1.9 %collective-permute-start.2 = (bf16[16,2688]{1,0:T(8,128)(2,1)S(1)}, bf16[16,2688]{1,0:T(8,128)(2,1)S(1)}, u32[]{:S(2)}, u32[]{:S(2)}) collective-permute-start(bf16[16,2688]{1,0:T(8,128)(2,1)S(1)} %shard_map.61.mine), channel_id=1, source_target_pairs={{0,4},{1,5},{2,6},{3,7},{4,0},{5,1},{6,2},{7,3},{8,12},{9,13},{10,... | collective-permute-start | bytes 258056 | tf_op jit(solution)/shard_map/ppermute | solution.py:280
  12.6 2.7 %collective-permute-done.2.other = bf16[16,2688]{1,0:T(8,128)(2,1)S(1)} collective-permute-done((bf16[16,2688]{1,0:T(8,128)(2,1)S(1)}, bf16[16,2688]{1,0:T(8,128)(2,1)S(1)}, u32[]{:S(2)}, u32[]{:S(2)}) %collective-permute-start.2) | collective-permute-done | bytes 86048 | tf_op jit(solution)/shard_map/ppermute | solution.py:280
  15.3 0.0 copy-start
  15.3 0.2 shard_map.62.mine
  15.5 2.9 %collective-permute-start.3 = (bf16[16,2688]{1,0:T(8,128)(2,1)S(1)}, bf16[16,2688]{1,0:T(8,128)(2,1)S(1)}, u32[]{:S(2)}, u32[]{:S(2)}) collective-permute-start(bf16[16,2688]{1,0:T(8,128)(2,1)S(1)} %shard_map.62.mine), channel_id=1, source_target_pairs={{0,8},{1,9},{2,10},{3,11},{4,12},{5,13},{6,14},{7,15},{8,0},{9,1},... | collective-permute-start | bytes 258056 | tf_op jit(solution)/shard_map/ppermute | solution.py:280
  18.4 0.0 collective-permute-start.7
  18.4 4.4 %collective-permute-start.8 = (bf16[48,2560]{1,0:T(8,128)(2,1)S(1)}, bf16[48,2560]{1,0:T(8,128)(2,1)S(1)}, u32[]{:S(2)}, u32[]{:S(2)}) collective-permute-start(bf16[48,2560]{1,0:T(8,128)(2,1)S(1)} %get-tuple-element.19), channel_id=1, source_target_pairs={{0,15},{1,2},{2,1},{3,4},{4,3},{5,6},{6,5},{7,8},{8,7},{9,10},{10,... | collective-permute-start | bytes 737288 | tf_op jit(solution)/shard_map/ppermute | solution.py:280
  22.8 0.0 collective-permute-done.3.other
  22.8 0.3 shard_map.63.mine
  23.1 0.1 collective-permute-start.4
  23.1 10.6 %collective-permute-done.4.other = bf16[16,2560]{1,0:T(8,128)(2,1)S(1)} collective-permute-done((bf16[16,2560]{1,0:T(8,128)(2,1)S(1)}, bf16[16,2560]{1,0:T(8,128)(2,1)S(1)}, u32[]{:S(2)}, u32[]{:S(2)}) %collective-permute-start.4) | collective-permute-done | bytes 81952 | tf_op jit(solution)/shard_map/ppermute | solution.py:280
  33.7 0.1 collective-permute-start.5
  33.8 0.0 collective-permute-done.7.refs_0_
  33.8 0.0 collective-permute-done.8.refs_1_
  33.8 0.0 collective-permute-done.6.near
  33.9 0.0 copy-done.1
  33.9 0.6 %shard_map.69.refs_4_ = bf16[128,640]{1,0:T(8,128)(2,1)S(1)} custom-call(s32[1]{0:T(128)} %bitcast.place, bf16[128,2560]{1,0:T(8,128)(2,1)S(1)} %bitcast.4, bf16[2,128,2560]{2,1,0:T(8,128)(2,1)S(1)} %get-tuple-element.16.kv, bf16[2,48,2560]{2,1,0:T(8,128)(2,1)S(1)} %collective-permute-done.6.near, bf16[48,2560]{1,0:T(8,128)(2,1)S(1)} %collective-permute-done.7.refs_0_, ...), custom_call_target="tpu_custom_call" | custom-call | flops 83886080 | bytes 983040 | tf_op jit(solution)/shard_map/pallas_call | solution.py:37
  34.5 0.6 %shard_map.68.refs_3_ = bf16[128,640]{1,0:T(8,128)(2,1)S(1)} custom-call(s32[1]{0:T(128)} %bitcast.place, bf16[128,2560]{1,0:T(8,128)(2,1)S(1)} %bitcast.5, bf16[2,128,2560]{2,1,0:T(8,128)(2,1)S(1)} %get-tuple-element.16.kv, bf16[2,48,2560]{2,1,0:T(8,128)(2,1)S(1)} %collective-permute-done.6.near, bf16[48,2560]{1,0:T(8,128)(2,1)S(1)} %collective-permute-done.7.refs_0_, ...), custom_call_target="tpu_custom_call" | custom-call | flops 83886080 | bytes 983040 | tf_op jit(solution)/shard_map/pallas_call | solution.py:37
  35.0 0.6 %shard_map.67.refs_2_ = bf16[128,640]{1,0:T(8,128)(2,1)S(1)} custom-call(s32[1]{0:T(128)} %bitcast.place, bf16[128,2560]{1,0:T(8,128)(2,1)S(1)} %bitcast.6, bf16[2,128,2560]{2,1,0:T(8,128)(2,1)S(1)} %get-tuple-element.16.kv, bf16[2,48,2560]{2,1,0:T(8,128)(2,1)S(1)} %collective-permute-done.6.near, bf16[48,2560]{1,0:T(8,128)(2,1)S(1)} %collective-permute-done.7.refs_0_, ...), custom_call_target="tpu_custom_call" | custom-call | flops 83886080 | bytes 983040 | tf_op jit(solution)/shard_map/pallas_call | solution.py:37
  35.6 0.6 %shard_map.66.refs_1_ = bf16[128,640]{1,0:T(8,128)(2,1)S(1)} custom-call(s32[1]{0:T(128)} %bitcast.place, bf16[128,2560]{1,0:T(8,128)(2,1)S(1)} %bitcast.7, bf16[2,128,2560]{2,1,0:T(8,128)(2,1)S(1)} %get-tuple-element.16.kv, bf16[2,48,2560]{2,1,0:T(8,128)(2,1)S(1)} %collective-permute-done.6.near, bf16[48,2560]{1,0:T(8,128)(2,1)S(1)} %collective-permute-done.7.refs_0_, ...), custom_call_target="tpu_custom_call" | custom-call | flops 83886080 | bytes 983040 | tf_op jit(solution)/shard_map/pallas_call | solution.py:37
  36.2 0.0 collective-permute-done.5.other
  36.2 0.0 copy-done
  36.2 3.7 %shard_map.70 = (bf16[128,2560]{1,0:T(8,128)(2,1)}, bf16[64,2560]{1,0:T(8,128)(2,1)}) custom-call(s32[1]{0:T(128)} %bitcast.place, bf16[32,2560]{1,0:T(8,128)(2,1)S(1)} %shard_map.64.mine, bf16[32,2560]{1,0:T(8,128)(2,1)S(1)} %collective-permute-done.5.other, bf16[2560,2560]{1,0:T(8,128)(2,1)S(1)} %copy-done, bf16[128,640]{1,0:T(8,128)(2,1)S(1)} %shard_map.66.refs_1_, ...), custom_call_target="tpu_custom_call" | custom-call | flops 2516582400 | bytes 13107200 | tf_op jit(solution)/shard_map/pallas_call | solution.py:37
  (1 shorter events, 0.0 us)
Async XLA Ops:
  2.9 1.6 %collective-permute-start = (bf16[32,2688]{1,0:T(8,128)(2,1)S(1)}, bf16[32,2688]{1,0:T(8,128)(2,1)S(1)}, u32[]{:S(2)}, u32[]{:S(2)}) collective-permute-start(bf16[32,2688]{1,0:T(8,128)(2,1)S(1)} %get-tuple-element.13), channel_id=1, source_target_pairs={{0,1},{1,0},{2,3},{3,2},{4,5},{5,4},{6,7},{7,6},{8,9},{9,8},{10,11... | collective-permute-start | bytes 516104 | tf_op jit(solution)/shard_map/ppermute | solution.py:280
  3.4 30.4 %copy-start.1 = (bf16[16,8,2560]{2,1,0:T(8,128)(2,1)S(1)}, bf16[16,8,2560]{2,1,0:T(8,128)(2,1)}, u32[]{:S(2)}) copy-start(bf16[16,8,2560]{2,1,0:T(8,128)(2,1)} %param.4) | copy-start | bytes 1966084
  3.8 30.0 %collective-permute-start.6 = (bf16[2,48,2560]{2,1,0:T(8,128)(2,1)S(1)}, bf16[2,48,2560]{2,1,0:T(8,128)(2,1)S(1)}, u32[]{:S(2)}, u32[]{:S(2)}) collective-permute-start(bf16[2,48,2560]{2,1,0:T(8,128)(2,1)S(1)} %get-tuple-element.17), channel_id=1, source_target_pairs={{0,1},{1,0},{2,3},{3,2},{4,5},{5,4},{6,7},{7,6},{8,9},{9,8},{10,11... | collective-permute-start | bytes 1474568 | tf_op jit(solution)/shard_map/ppermute | solution.py:280
  4.8 5.8 %collective-permute-start.1 = (bf16[16,2688]{1,0:T(8,128)(2,1)S(1)}, bf16[16,2688]{1,0:T(8,128)(2,1)S(1)}, u32[]{:S(2)}, u32[]{:S(2)}) collective-permute-start(bf16[16,2688]{1,0:T(8,128)(2,1)S(1)} %get-tuple-element.15), channel_id=1, source_target_pairs={{0,2},{1,3},{2,0},{3,1},{4,6},{5,7},{6,4},{7,5},{8,10},{9,11},{10,... | collective-permute-start | bytes 258056 | tf_op jit(solution)/shard_map/ppermute | solution.py:280
  10.7 4.6 %collective-permute-start.2 = (bf16[16,2688]{1,0:T(8,128)(2,1)S(1)}, bf16[16,2688]{1,0:T(8,128)(2,1)S(1)}, u32[]{:S(2)}, u32[]{:S(2)}) collective-permute-start(bf16[16,2688]{1,0:T(8,128)(2,1)S(1)} %shard_map.61.mine), channel_id=1, source_target_pairs={{0,4},{1,5},{2,6},{3,7},{4,0},{5,1},{6,2},{7,3},{8,12},{9,13},{10,... | collective-permute-start | bytes 258056 | tf_op jit(solution)/shard_map/ppermute | solution.py:280
  15.3 20.9 %copy-start = (bf16[2560,2560]{1,0:T(8,128)(2,1)S(1)}, bf16[2560,2560]{1,0:T(8,128)(2,1)}, u32[]{:S(2)}) copy-start(bf16[2560,2560]{1,0:T(8,128)(2,1)} %refs_0_.1) | copy-start | bytes 39321604
  15.5 7.3 %collective-permute-start.3 = (bf16[16,2688]{1,0:T(8,128)(2,1)S(1)}, bf16[16,2688]{1,0:T(8,128)(2,1)S(1)}, u32[]{:S(2)}, u32[]{:S(2)}) collective-permute-start(bf16[16,2688]{1,0:T(8,128)(2,1)S(1)} %shard_map.62.mine), channel_id=1, source_target_pairs={{0,8},{1,9},{2,10},{3,11},{4,12},{5,13},{6,14},{7,15},{8,0},{9,1},... | collective-permute-start | bytes 258056 | tf_op jit(solution)/shard_map/ppermute | solution.py:280
  18.4 15.5 %collective-permute-start.7 = (bf16[48,2560]{1,0:T(8,128)(2,1)S(1)}, bf16[48,2560]{1,0:T(8,128)(2,1)S(1)}, u32[]{:S(2)}, u32[]{:S(2)}) collective-permute-start(bf16[48,2560]{1,0:T(8,128)(2,1)S(1)} %get-tuple-element.18), channel_id=1, source_target_pairs={{0,15},{1,2},{2,1},{3,4},{4,3},{5,6},{6,5},{7,8},{8,7},{9,10},{10,... | collective-permute-start | bytes 737288 | tf_op jit(solution)/shard_map/ppermute | solution.py:280
  18.4 15.5 %collective-permute-start.8 = (bf16[48,2560]{1,0:T(8,128)(2,1)S(1)}, bf16[48,2560]{1,0:T(8,128)(2,1)S(1)}, u32[]{:S(2)}, u32[]{:S(2)}) collective-permute-start(bf16[48,2560]{1,0:T(8,128)(2,1)S(1)} %get-tuple-element.19), channel_id=1, source_target_pairs={{0,15},{1,2},{2,1},{3,4},{4,3},{5,6},{6,5},{7,8},{8,7},{9,10},{10,... | collective-permute-start | bytes 737288 | tf_op jit(solution)/shard_map/ppermute | solution.py:280
  23.1 10.6 %collective-permute-start.4 = (bf16[16,2560]{1,0:T(8,128)(2,1)S(1)}, bf16[16,2560]{1,0:T(8,128)(2,1)S(1)}, u32[]{:S(2)}, u32[]{:S(2)}) collective-permute-start(bf16[16,2560]{1,0:T(8,128)(2,1)S(1)} %shard_map.63.mine), channel_id=1, source_target_pairs={{0,2},{1,3},{2,0},{3,1},{4,6},{5,7},{6,4},{7,5},{8,10},{9,11},{10,... | collective-permute-start | bytes 245768 | tf_op jit(solution)/shard_map/ppermute | solution.py:280
  33.7 2.5 %collective-permute-start.5 = (bf16[32,2560]{1,0:T(8,128)(2,1)S(1)}, bf16[32,2560]{1,0:T(8,128)(2,1)S(1)}, u32[]{:S(2)}, u32[]{:S(2)}) collective-permute-start(bf16[32,2560]{1,0:T(8,128)(2,1)S(1)} %shard_map.64.mine), channel_id=1, source_target_pairs={{0,1},{1,0},{2,3},{3,2},{4,5},{5,4},{6,7},{7,6},{8,9},{9,8},{10,11... | collective-permute-start | bytes 491528 | tf_op jit(solution)/shard_map/ppermute | solution.py:280
